TPU v7x, 32 devices: a whole 2x2x4 slice. The times are simulated.
32 devices in a mesh: groups: 2 (over y), sky: 4 (over z), shell: 2 (over x), sub: 2 (over core).
Axes of the slice: x: 2, y: 2, z: 4, core: 2. Of those that a mesh axis runs over, the one named last changes fastest.
Arguments:
- part_cycle: int32 [2, 2048, 256], P('shell', ('sky', 'sub')), may hold values from 0 to 1
- part_pixel: int32 [2, 2048, 256], P('shell', ('sky', 'sub')), may hold values from 0 to 127
- part_mass: float32 [2, 2048, 256], P('shell', ('sky', 'sub')), may hold values from 0.3 to 3
- tile_block: int32 [2, 2048, 1], P('shell', ('sky', 'sub')), may hold values from 0 to 7; in each aligned block of 256 rows (0 to 255, 256 to 511, ..., all dimensions but the last counted through in order) at most 128 rows name the same one
- tile_shell: int32 [2, 2048], P('shell', ('sky', 'sub')), may hold values from 0 to 1
- tile_pixel: int32 [2, 2048], P('shell', ('sky', 'sub')), may hold values from 0 to 63
- harmonic_basis: bfloat16 [128, 16, 4096], P('sky', 'sub'), may hold values from -1.5 to 1.5
- lens_weight: float32 [4, 4], replicated, may hold values from 0.2 to 1
Outputs:
- convergence: float32 [8, 128, 2, 4096], P(('groups', 'shell'), 'sky', None, 'sub'), parts along dimension 0
There are 2 independent parts, one for each index of `groups`. A program takes and returns all parts, laid end to end along the dimension named above; an argument that names none is the same for every part. Nothing has to cross between parts.
Inputs may be any that keep to these rules, and one draw needn't show every extreme that they name: `tile_block`: among the rows of one device no cycle block is named by more than 128 tiles, and in some device one block is named by exactly 128.
All inputs are finite; a program needn't handle non-finite values.
Results may differ from a plain program's by a relative error of at most 0.0015.
Values may be sent and summed in bfloat16 or wider, within the bound.
No kernel may reach another device: no remote copies, remote signals or barrier semaphores. Data moves between devices by JAX's collectives and lax.ppermute only.
A program may use at most 192 MiB of HBM per device.

v0:
```python
import math

import jax
import jax.numpy as jnp
from jax import lax
from jax.sharding import PartitionSpec as P

NP = 8192
M = 128
TP = 128
CYCLE_DEV = 2
SHELL_DEV = 2


precise = lax.Precision.HIGHEST


def deposit(cycle_index, pixel_index, masses):
    cycle_axis = jnp.arange(CYCLE_DEV, dtype=jnp.float32)
    pixel_axis = jnp.arange(TP, dtype=jnp.float32)
    cycle_part = jnp.exp(
        -0.5 * (cycle_axis[None, None, :] - cycle_index.astype(jnp.float32)[:, :, None]) ** 2
    )
    pixel_part = jnp.exp(
        -((pixel_axis[None, None, :] - pixel_index.astype(jnp.float32)[:, :, None]) ** 2) / 18.0
    )
    weighted = pixel_part * masses[:, :, None]
    return jnp.einsum("tpk,tpj->tkj", cycle_part, weighted, precision=precise)


def fourier_table(count):
    pixels = jnp.arange(count, dtype=jnp.int32)
    orders = jnp.arange(M, dtype=jnp.int32)
    phases = pixels[:, None] * orders[None, :] % NP
    angles = phases.astype(jnp.float32) * (2.0 * math.pi / NP)
    return jnp.concatenate([jnp.cos(angles), -jnp.sin(angles)], axis=1)


def body(
    part_cycle,
    part_pixel,
    part_mass,
    tile_block,
    tile_shell,
    tile_pixel,
    harmonic_basis,
    lens_weight,
):
    sky_count = lax.axis_size("sky")
    sub_count = lax.axis_size("sub")
    owners = sky_count * sub_count
    tile_count = part_cycle.shape[1]
    tile_sums = deposit(part_cycle[0], part_pixel[0], part_mass[0]).reshape(
        tile_count, CYCLE_DEV * TP
    )
    local_modes = jnp.dot(
        tile_sums.reshape(tile_count * CYCLE_DEV, TP), fourier_table(TP), precision=precise
    )
    local_modes = local_modes.reshape(tile_count, CYCLE_DEV, 2, M)
    orders = jnp.arange(M, dtype=jnp.int32)
    turns = tile_pixel[0][:, None] * TP * orders[None, :] % NP
    angles = turns.astype(jnp.float32) * (2.0 * math.pi / NP)
    cosine = jnp.cos(angles)[:, None, :]
    sine = -jnp.sin(angles)[:, None, :]
    real_part = local_modes[:, :, 0, :]
    imag_part = local_modes[:, :, 1, :]
    rotated = jnp.stack(
        [real_part * cosine - imag_part * sine, real_part * sine + imag_part * cosine], axis=2
    )
    bin_key = tile_shell[0] * owners + tile_block[0, :, 0]
    bin_hot = (bin_key[None, :] == jnp.arange(SHELL_DEV * owners, dtype=jnp.int32)[:, None]).astype(
        jnp.float32
    )
    binned = jnp.dot(bin_hot, rotated.reshape(tile_count, CYCLE_DEV * 2 * M), precision=precise)
    binned = binned.reshape(SHELL_DEV, owners, CYCLE_DEV, 2, M).transpose(4, 0, 3, 1, 2)
    binned = binned.reshape(M, SHELL_DEV, 2, owners * CYCLE_DEV)
    order_part = lax.psum_scatter(binned, "sky", scatter_dimension=0, tiled=True)
    cycle_part = lax.psum_scatter(order_part, "sub", scatter_dimension=3, tiled=True)
    by_order = (cycle_part * (2.0 * math.pi / NP)).astype(jnp.bfloat16)
    harmonics = jnp.einsum(
        "mrl,mscr->mscl", harmonic_basis, by_order, preferred_element_type=jnp.float32
    )
    halves = lax.psum_scatter(harmonics, "sub", scatter_dimension=3, tiled=True)
    shell_index = lax.axis_index("shell")
    sources = lens_weight.shape[0]
    first_shell = shell_index * SHELL_DEV
    local_weight = lax.dynamic_slice_in_dim(lens_weight, first_shell, SHELL_DEV, 1)
    source_ids = jnp.arange(sources, dtype=jnp.int32)
    shell_ids = first_shell + jnp.arange(SHELL_DEV, dtype=jnp.int32)
    local_weight = local_weight * (shell_ids[None, :] <= source_ids[:, None]).astype(jnp.float32)
    planes = jnp.einsum("js,mscl->jmcl", local_weight, halves, precision=precise)
    per_device = sources // lax.axis_size("shell")
    totals = lax.psum(planes, "shell")
    result = lax.dynamic_slice_in_dim(totals, shell_index * per_device, per_device, 0)
    return result


def solution(mesh):
    return jax.shard_map(
        body,
        mesh=mesh,
        in_specs=(
            P("shell", ("sky", "sub"), None),
            P("shell", ("sky", "sub"), None),
            P("shell", ("sky", "sub"), None),
            P("shell", ("sky", "sub"), None),
            P("shell", ("sky", "sub")),
            P("shell", ("sky", "sub")),
            P("sky", "sub", None),
            P(),
        ),
        out_specs=P(("groups", "shell"), "sky", None, "sub"),
        check_vma=False,
    )
```

profile of v0, /device:TPU:0, one launch (start us, length us, event | category | flops | bytes accessed | tf_op | source)
XLA Modules:
  0.0 695.7 jit_solution(14472158354454681368)
XLA Ops:
  6.5 0.3 sine_negate_fusion.1
  6.8 0.8 broadcast_multiply_fusion
  7.7 0.5 fusion.38
  8.2 0.0 copy-start.2
  8.2 1.1 convert_bitcast_fusion
  9.3 35.0 %fusion.15 = f32[256,2,128,1]{2,1,0,3:T(2,128)S(1)} fusion(f32[256,256]{1,0:T(8,128)} %bitcast.57, f32[256,256]{1,0:T(8,128)S(1)} %get-tuple-element.11, f32[256,256]{1,0:T(8,128)S(1)} %get-tuple-element.12), kind=kOutput, calls=%fused_computation.15 | convolution fusion | flops 243662848 | bytes 1048576 | tf_op jit(solution)/shard_map/tpk,tpj->tkj/dot_general | solution.py:28
  44.4 0.6 fusion.25
  45.0 0.1 multiply_subtract_fusion
  45.1 0.3 convolution_bitcast_fusion
  45.5 0.7 copy.30
  46.2 0.0 reduce-scatter.10.cloned.1.call-update
  46.2 0.0 reduce-scatter.8.cloned.1.call-start
  46.3 22.1 %reduce-scatter.10.cloned.1.call-done = f32[32,64]{1,0:T(8,128)} async-done(((f32[128,64]{1,0:T(8,128)}), f32[32,64]{1,0:T(8,128)}) %reduce-scatter.10.cloned.1.call-update) | async-done | bytes 8208
  68.4 1.4 copy.31
  69.8 0.0 reduce-scatter.8.cloned.1.call-update
  69.8 0.0 reduce-scatter.12.cloned.1.call-start
  69.8 6.4 reduce-scatter.8.cloned.1.call-done
  76.3 0.7 multiply_convert_fusion
  77.0 0.1 copy.16
  77.1 2.1 fusion.13
  79.2 139.1 %copy.28 = f32[32,2,2,4096]{1,2,0,3:T(2,128)} copy(f32[32,2,2,4096]{3,1,2,0:T(2,128)} %fusion.13) | data formatting | bytes 4194304
  218.3 165.9 %reshape.116 = f32[4096,128]{1,0:T(8,128)} reshape(f32[4096,32,2,2]{3,2,1,0:T(2,128)} %bitcast.23) | data formatting | bytes 4194304
  384.2 0.0 reduce-scatter.12.cloned.1.call-update
  384.2 0.0 all-reduce.2.cloned.1.call-start
  384.3 0.0 copy-start.1
  384.3 11.0 %reduce-scatter.12.cloned.1.call-done = f32[2048,128]{1,0:T(8,128)} async-done(((f32[4096,128]{1,0:T(8,128)}), f32[2048,128]{1,0:T(8,128)}) %reduce-scatter.12.cloned.1.call-update) | async-done | bytes 1048592
  395.2 105.0 %reshape.117 = f32[2048,32,2,2]{3,2,1,0:T(2,128)} reshape(f32[2048,128]{1,0:T(8,128)} %reduce-scatter.12.cloned.1.call-done) | data formatting | bytes 2097152
  500.2 120.6 %fusion = f32[4,32,2,2048]{3,0,2,1:T(4,128)} fusion(f32[32,2,2,2048]{1,2,0,3:T(2,128)} %bitcast.24, f32[4,4]{1,0:T(4,128)S(1)} %copy-done.1, s32[]{:T(128)S(6)} %select_n.26, s32[2]{0:T(128)S(1)} %iota_add_fusion), kind=kOutput, calls=%fused_computation | convolution fusion | flops 12582928 | bytes 3145804 | tf_op jit(solution)/shard_map/js,mscl->jmcl/dot_general | solution.py:91
  620.8 0.0 all-reduce.2.cloned.1.call-update
  620.8 64.4 %all-reduce.2.cloned.1.call-done = f32[4,32,2,2048]{3,0,2,1:T(4,128)} async-done(((f32[4,32,2,2048]{3,0,2,1:T(4,128)}), f32[4,32,2,2048]{3,0,2,1:T(4,128)}) %all-reduce.2.cloned.1.call-update) | async-done | bytes 2097168 | tf_op jit(solution)/shard_map/psum | solution.py:93
  685.2 2.2 constant_dynamic-slice_fusion
  687.4 1.8 copy.18
  (12 shorter events, 0.1 us)
Async XLA Ops:
  6.5 70.6 %copy-start = (bf16[32,8,4096]{2,1,0:T(8,128)(2,1)S(1)}, bf16[32,8,4096]{2,1,0:T(8,128)(2,1)}, u32[]{:S(2)}) copy-start(bf16[32,8,4096]{2,1,0:T(8,128)(2,1)} %param.14) | copy-start | bytes 6291460
  6.5 61.8 %reduce-scatter.10.cloned.1.call-start = ((), (), s32[]{:S(2)}) async-start(), calls=%async_computation.5 | async-start | bytes 81920
  8.2 36.8 %copy-start.2 = (s32[1,256,1]{1,2,0:T(1,128)S(1)}, s32[1,256,1]{1,2,0:T(1,128)}, u32[]{:S(2)}) copy-start(s32[1,256,1]{1,2,0:T(1,128)} %param.11) | copy-start | bytes 3076
  8.2 36.8 %copy-start.3 = (s32[1,256]{1,0:T(1,128)S(1)}, s32[1,256]{1,0:T(1,128)}, u32[]{:S(2)}) copy-start(s32[1,256]{1,0:T(1,128)} %param.12) | copy-start | bytes 3076
  46.2 30.1 %reduce-scatter.8.cloned.1.call-start = ((), (), s32[]{:S(2)}) async-start(), calls=%async_computation.3 | async-start | bytes 49152 | tf_op jit(solution)/shard_map/reduce_scatter | solution.py:78
  69.8 325.4 %reduce-scatter.12.cloned.1.call-start = ((), (), s32[]{:S(2)}) async-start(), calls=%async_computation.6 | async-start | bytes 3145728
  384.2 301.0 %all-reduce.2.cloned.1.call-start = ((), (), s32[]{:S(2)}) async-start(), calls=%async_computation.4 | async-start | bytes 4194304 | tf_op jit(solution)/shard_map/psum | solution.py:93
  384.3 115.9 %copy-start.1 = (f32[4,4]{1,0:T(4,128)S(1)}, f32[4,4]{1,0:T(4,128)}, u32[]{:S(2)}) copy-start(f32[4,4]{1,0:T(4,128)} %param.15) | copy-start | bytes 196
Sparse Core Ops, SparseCore 0:
  46.3 21.9 reduce-scatter.9
  70.5 5.6 reduce-scatter.7
  384.3 10.8 reduce-scatter.11
  620.9 64.2 all-reduce.1
where the time goes:
time: 706 us; the launch traced here: 696 us
  local copies, waits for them, and re-layouts  416 us (59%)
  matrix products  159 us (23%)
  waiting for transfers between devices  104 us (15%)
  between operations  13.3 us (2%)
    unnamed x13, local copies, waits for them, and re-layouts  412 us
    dot_general x1, matrix products, body(): jnp.einsum('js,mscl->jmcl', local_weight, halves, precision=precise)  121 us
    psum x1, waiting for transfers between devices, body(): totals = lax.psum(planes, 'shell')  64.4 us
    dot_general x1, matrix products, deposit(): return jnp.einsum('tpk,tpj->tkj', cycle_part, weighted, precision=precise)  35 us
    unnamed x6, waiting for transfers between devices  33.1 us
  transfers between devices with their start and end apart: 4, of which 4 were waited for; matrix products, arithmetic and copies ran while one was open for 0% of the time, Pallas kernels for 0%

commit v1 on v0

v1 whole, which is shorter than its diff:
```python
import functools
import math

import jax
import jax.numpy as jnp
import numpy as np
from jax import lax
from jax.experimental import pallas as pl
from jax.experimental.pallas import tpu as pltpu
from jax.sharding import PartitionSpec as P

NP = 8192
M = 128
TP = 128
CYCLE_DEV = 2
SHELL_DEV = 2

f32 = jnp.float32
bf16 = jnp.bfloat16


def split(x):
    high = x.astype(bf16)
    return high, (x - high.astype(f32)).astype(bf16)


def dot(a, b, contract=((1,), (0,))):
    return lax.dot_general(a, b, (contract, ((), ())), preferred_element_type=f32)


def split_np(x):
    high = x.astype(np.float32).astype(bf16)
    return np.stack([high, (x - high.astype(np.float64)).astype(np.float32).astype(bf16)])


@functools.cache
def tables(sky):
    part = np.tile(np.arange(2), M)
    order = np.repeat(np.arange(M), 2)
    pixel = np.arange(TP)
    spread = np.exp(-((pixel[:, None] - pixel[None, :]) ** 2) / 18.0)
    angle = (pixel[:, None] * order[None, :] % NP) * (2.0 * math.pi / NP)
    wave = np.where(part == 0, np.cos(angle), -np.sin(angle))
    other = np.where(part == 0, -np.sin(angle), np.cos(angle))
    modes = split_np(spread @ np.concatenate([wave, other], 1))
    place = np.arange(NP // TP)
    turn = (place[:, None] * TP * order[None, :] % NP) * (2.0 * math.pi / NP)
    cosine, sine = np.cos(turn), -np.sin(turn)
    phase = split_np(np.concatenate([cosine, np.where(part == 0, -sine, sine)], 1))
    return modes, phase


def deposit_kernel(cyc, pix, mass, block, shell, place, modes_tab, phase_tab, out, h, *, blocks):
    tiles, count = cyc.shape[1:]
    columns = 2 * M
    faint = math.exp(-0.5)
    rows = lax.broadcasted_iota(jnp.int32, (TP, count), 0)
    row = lax.broadcasted_iota(jnp.int32, (8, TP), 0)

    def group(g, carry):
        at = pl.ds(pl.multiple_of(g * 8, 8), 8)
        c8, x8, m8 = cyc[0, at, :], pix[0, at, :], mass[0, at, :]
        far = m8 * faint
        w0, w1 = jnp.where(c8 == 0, m8, far), jnp.where(c8 == 0, far, m8)
        a0, b0 = split(w0)
        a1, b1 = split(w1)
        left = jnp.concatenate([x.astype(f32) for x in (a0, a1, b0, b1)], 0).astype(bf16)
        h0 = jnp.zeros((8, TP), f32)
        h1 = jnp.zeros((8, TP), f32)
        for t in range(8):
            hot = jnp.where(rows == x8[t : t + 1, :], 1.0, 0.0).astype(bf16)
            got = dot(left, hot, ((1,), (1,)))
            h0 = jnp.where(row == t, got[0:8] + got[16:24], h0)
            h1 = jnp.where(row == t, got[8:16] + got[24:32], h1)
        h[0, at, :] = h0
        h[1, at, :] = h1
        return carry

    lax.fori_loop(0, tiles // 8, group, 0)

    places = phase_tab.shape[1]
    hot_place = jnp.where(
        lax.broadcasted_iota(jnp.int32, (places, tiles), 0) == place[...], 1.0, 0.0
    ).astype(bf16)
    phase = dot(hot_place, phase_tab[0], ((0,), (0,))) + dot(hot_place, phase_tab[1], ((0,), (0,)))
    bins = SHELL_DEV * blocks
    key = shell[...] * blocks + block[...]
    hot_bin = jnp.where(
        lax.broadcasted_iota(jnp.int32, (bins, tiles), 0) == key, 1.0, 0.0
    ).astype(bf16)
    for k in range(CYCLE_DEV):
        high, low = split(h[k])
        modes = dot(high, modes_tab[0]) + dot(high, modes_tab[1]) + dot(low, modes_tab[0])
        turned = modes[:, :columns] * phase[:, :columns] + modes[:, columns:] * phase[:, columns:]
        high, low = split(turned)
        out[k] = dot(hot_bin, high) + dot(hot_bin, low)


def legendre_kernel(where, recv, weight, own, other, out, left, *, blocks):
    lanes = recv.shape[-1]
    orders = own.shape[0]
    cycles = own.shape[1]
    width = orders * cycles
    half = lanes // CYCLE_DEV
    planes = out.shape[0]

    @pl.when(pl.program_id(0) == 0)
    def _():
        sub, first = where[0], where[1] * planes
        maps = []
        for x in range(recv.shape[0]):
            total = recv[x, 0]
            for i in range(1, recv.shape[1]):
                total = total + recv[x, i]
            total = (total * (2.0 * math.pi / NP)).astype(bf16).astype(f32)
            maps += [total[s * blocks : (s + 1) * blocks] for s in range(SHELL_DEV)]
        column = lax.broadcasted_iota(jnp.int32, (blocks, width), 1)
        row = lax.broadcasted_iota(jnp.int32, (blocks, width), 0)
        wide = lax.broadcasted_iota(jnp.int32, (half, width), 1)
        keep = lax.broadcasted_iota(jnp.int32, (half, width), 0) // 2 == wide // cycles
        even = wide % CYCLE_DEV == 0
        for side in range(2):
            mine = sub if side == 0 else 1 - sub
            cycle = mine * cycles + column % cycles
            spread = jnp.where(row == cycle // CYCLE_DEV, 1.0, 0.0).astype(bf16)
            for i in range(planes):
                total = jnp.zeros((blocks, lanes), f32)
                for s, value in enumerate(maps):
                    factor = jnp.where(s <= first + i, weight[first + i, s], 0.0)
                    total = total + factor * value
                high, low = split(total)
                for j, piece in enumerate((high, low)):
                    grown = dot(piece, spread, ((0,), (0,)))
                    grown = jnp.where(even, grown[:half], grown[half:])
                    grown = jnp.where(keep, grown, 0.0).astype(bf16)
                    start = (j * planes + i) * half
                    left[side, start : start + half, :] = grown

    span = out.shape[-1]
    a = own[...].reshape(width, span)
    b = other[...].reshape(width, span)
    result = dot(left[0], a) + dot(left[1], b)
    result = result[: planes * half] + result[planes * half :]
    for i in range(planes):
        for m in range(orders):
            start = i * half + m * 2
            out[i, m, :, :] = result[start : start + 2, :]


def body(part_cycle, part_pixel, part_mass, tile_block, tile_shell, tile_pixel, basis, lens_weight):
    sky, sub, shells = lax.axis_size("sky"), lax.axis_size("sub"), lax.axis_size("shell")
    tiles, count = part_cycle.shape[1:]
    orders, cycles, degrees = basis.shape
    blocks = cycles * sub // CYCLE_DEV
    sources = lens_weight.shape[0] // shells
    columns = 2 * M
    modes_tab, phase_tab = tables(sky)

    other = lax.ppermute(basis, "sub", [(i, (i + 1) % sub) for i in range(sub)])

    binned = pl.pallas_call(
        functools.partial(deposit_kernel, blocks=blocks),
        out_shape=jax.ShapeDtypeStruct((CYCLE_DEV, SHELL_DEV * blocks, columns), f32),
        scratch_shapes=[pltpu.VMEM((CYCLE_DEV, tiles, TP), f32)],
        name="deposit",
    )(
        part_cycle,
        part_pixel,
        part_mass,
        tile_block.reshape(1, tiles),
        tile_shell,
        tile_pixel,
        jnp.asarray(modes_tab),
        jnp.asarray(phase_tab),
    )
    lanes = CYCLE_DEV * orders * 2
    send = binned.reshape(CYCLE_DEV, SHELL_DEV * blocks, sky, orders * 2).transpose(2, 1, 0, 3)
    send = send.reshape(sky, 1, SHELL_DEV * blocks, lanes)
    send = jnp.broadcast_to(send, (sky, shells * sub, SHELL_DEV * blocks, lanes))
    send = send.reshape(sky * shells * sub, SHELL_DEV * blocks, lanes)
    recv = lax.all_to_all(send, ("sky", "shell", "sub"), 0, 0, tiled=True)
    recv = recv.reshape(sky, shells, sub, SHELL_DEV * blocks, lanes).transpose(1, 0, 2, 3, 4)
    recv = recv.reshape(shells, sky * sub, SHELL_DEV * blocks, lanes)

    where = jnp.stack([lax.axis_index("sub"), lax.axis_index("shell")]).astype(jnp.int32)
    own_degrees = degrees // sub
    span = min(own_degrees, 512)
    steps = own_degrees // span
    half = orders * 2
    return pl.pallas_call(
        functools.partial(legendre_kernel, blocks=blocks),
        out_shape=jax.ShapeDtypeStruct((sources, orders, 2, own_degrees), f32),
        grid_spec=pltpu.PrefetchScalarGridSpec(
            num_scalar_prefetch=1,
            grid=(steps,),
            in_specs=[
                pl.BlockSpec(recv.shape, lambda j, w: (0, 0, 0, 0)),
                pl.BlockSpec(memory_space=pltpu.SMEM),
                pl.BlockSpec((orders, cycles, span), lambda j, w: (0, 0, w[0] * steps + j)),
                pl.BlockSpec((orders, cycles, span), lambda j, w: (0, 0, w[0] * steps + j)),
            ],
            out_specs=pl.BlockSpec((sources, orders, 2, span), lambda j, w: (0, 0, 0, j)),
            scratch_shapes=[pltpu.VMEM((2, 2 * sources * half, orders * cycles), bf16)],
        ),
        name="legendre",
    )(where, recv, lens_weight, basis, other)


def solution(mesh):
    return jax.shard_map(
        body,
        mesh=mesh,
        in_specs=(
            P("shell", ("sky", "sub"), None),
            P("shell", ("sky", "sub"), None),
            P("shell", ("sky", "sub"), None),
            P("shell", ("sky", "sub"), None),
            P("shell", ("sky", "sub")),
            P("shell", ("sky", "sub")),
            P("sky", "sub", None),
            P(),
        ),
        out_specs=P(("groups", "shell"), "sky", None, "sub"),
        check_vma=False,
    )
```

time: 706 us -> 36.5 us (0.05); the launches traced: 696 us -> 36.1 us
  local copies, waits for them, and re-layouts: 416 us -> 3.66 us
  matrix products: 159 us -> 0 us
  waiting for transfers between devices: 104 us -> 7.25 us
  Pallas kernels: 0 us -> 17.1 us
  between operations: 13.3 us -> 0.03 us
  starting transfers between devices: 0.13 us -> 7.48 us
    unnamed x13 -> x2, local copies, waits for them, and re-layouts: 412 us -> 1.33 us
    dot_general x5 -> x0, matrix products: 159 us -> none  [the longest x1 121 us: body(): jnp.einsum('js,mscl->jmcl', local_weight, halves, precision=precise)]
    psum x1 -> x0, waiting for transfers between devices: 64.4 us -> none  [body(): totals = lax.psum(planes, 'shell')]
    unnamed x6 -> x0, waiting for transfers between devices: 33.1 us -> none
    pallas_call x0 -> x2, Pallas kernels: none -> 17.1 us  [the longest x1 11.9 us: body(): pl.pallas_call(functools.partial(deposit_kernel, blocks=blocks), out_shap...]
    all_to_all x0 -> x1, waiting for transfers between devices: none -> 7.25 us  [body(): recv = lax.all_to_all(send, ('sky', 'shell', 'sub'), 0, 0, tiled=True)]
  transfers between devices with their start and end apart: 4 -> 2, of which waited for: 4 -> 1; matrix products, arithmetic and copies ran while one was open for 0% -> 8% of each run, Pallas kernels for 0% -> 33%
where the time goes in v1:
time: 36.5 us; the launch traced here: 36.1 us
  Pallas kernels  17.1 us (47%)
  starting transfers between devices  7.48 us (20%)
  waiting for transfers between devices  7.25 us (20%)
  local copies, waits for them, and re-layouts  3.66 us (10%)
  other arithmetic  0.65 us (2%)
    pallas_call x1, Pallas kernels, body(): pl.pallas_call(functools.partial(deposit_kernel, blocks=blocks), out_shap...  11.9 us
    all_to_all x1, waiting for transfers between devices, body(): recv = lax.all_to_all(send, ('sky', 'shell', 'sub'), 0, 0, tiled=True)  7.25 us
    all_to_all x1, starting transfers between devices, body(): recv = lax.all_to_all(send, ('sky', 'shell', 'sub'), 0, 0, tiled=True)  6.99 us
    pallas_call x1, Pallas kernels, body(): pl.pallas_call(functools.partial(legendre_kernel, blocks=blocks), out_sha...  5.22 us
    unnamed x2, local copies, waits for them, and re-layouts  1.33 us
    reshape x2, local copies, waits for them, and re-layouts, body(): binned.reshape(CYCLE_DEV, SHELL_DEV * blocks, sky, orders * 2)  0.9 us
    broadcast_in_dim x2, local copies, waits for them, and re-layouts, body(): jnp.broadcast_to(send, (sky, shells * sub, SHELL_DEV * blocks, lanes))  0.77 us
  transfers between devices with their start and end apart: 2, of which 1 were waited for; matrix products, arithmetic and copies ran while one was open for 8% of the time, Pallas kernels for 33%

profile of v1, /device:TPU:0, one launch (start us, length us, event | category | flops | bytes accessed | tf_op | source)
XLA Modules:
  0.0 36.1 jit_solution(9680432926475941000)
XLA Ops:
  0.0 0.5 %collective-permute-start = (bf16[32,8,4096]{2,1,0:T(8,128)(2,1)}, bf16[32,8,4096]{2,1,0:T(8,128)(2,1)S(1)}, u32[]{:S(2)}, u32[]{:S(2)}) collective-permute-start(bf16[32,8,4096]{2,1,0:T(8,128)(2,1)} %own.1), channel_id=1, source_target_pairs={{0,1},{1,0},{2,3},{3,2},{4,5},{5,4},{6,7},{7,6},{8,9},{9,8},{10,11... | collective-permute-start | bytes 6291464 | tf_op jit(solution)/shard_map/ppermute | solution.py:159
  0.5 11.9 %deposit.1 = f32[2,16,256]{2,1,0:T(8,128)} custom-call(s32[1,256,256]{2,1,0:T(8,128)} %cyc.1, s32[1,256,256]{2,1,0:T(8,128)} %pix.1, f32[1,256,256]{2,1,0:T(8,128)} %mass.1, s32[1,256]{1,0:T(1,128)} %bitcast.14, s32[1,256]{1,0:T(1,128)} %shell.1, s32[1,256]{1,0:T(1,128)} %place.1, bf16[2,128,512]{2,1,0:T(8,128)(2,1)} %constant.10.clone.modes_tab, ...), custom_call_target="tpu_custom_call" | custom-call | tf_op jit(solution)/shard_map/deposit/pallas_call | solution.py:161
  12.4 0.8 %reshape.18 = f32[2,16,4,64]{3,2,1,0:T(4,128)S(1)} reshape(f32[2,16,256]{2,1,0:T(8,128)} %deposit.1) | data formatting | bytes 65536 | tf_op jit(solution)/shard_map/reshape | solution.py:177
  13.2 0.1 copy.14
  13.3 0.1 broadcast_in_dim.7
  13.4 0.7 %broadcast_in_dim.8 = f32[4,4,16,128]{3,2,1,0:T(8,128)} broadcast(f32[4,16,128]{2,1,0:T(8,128)S(1)} %broadcast_in_dim.7), dimensions={0,2,3} | broadcast | bytes 163840 | tf_op jit(solution)/shard_map/broadcast_in_dim | solution.py:179
  14.0 7.0 %all-to-all-start = ((f32[16,16,128]{2,1,0:T(8,128)}), f32[16,16,128]{2,1,0:T(8,128)S(1)}, u32[]{:S(2)}, u32[]{:S(2)}) async-start(f32[16,16,128]{2,1,0:T(8,128)} %bitcast.4), calls=%async_computation | async-start | bytes 262144 | tf_op jit(solution)/shard_map/all_to_all | solution.py:181
  21.0 0.7 %pad_add_fusion.where = s32[2]{0:T(128)} fusion(s32[1]{0:T(128)} %bitcast.1, s32[1]{0:T(128)} %bitcast), kind=kLoop, calls=%fused_computation.1 | loop fusion | flops 2 | bytes 16 | tf_op jit(solution)/shard_map/stack | solution.py:185
  21.7 7.2 %all-to-all-done = f32[16,16,128]{2,1,0:T(8,128)S(1)} async-done(((f32[16,16,128]{2,1,0:T(8,128)}), f32[16,16,128]{2,1,0:T(8,128)S(1)}, u32[]{:S(2)}, u32[]{:S(2)}) %all-to-all-start) | async-done | bytes 131104 | tf_op jit(solution)/shard_map/all_to_all | solution.py:181
  28.9 0.7 %copy.12 = f32[2,4,2,16,128]{4,3,2,1,0:T(8,128)} copy(f32[2,4,2,16,128]{4,3,2,0,1:T(8,128)S(1)} %bitcast.12) | data formatting | bytes 262144 | tf_op jit(solution)/shard_map/transpose | solution.py:182
  29.6 0.0 collective-permute-done.other
  29.6 0.0 copy-start
  29.6 1.3 %copy-done = bf16[32,8,4096]{2,1,0:T(8,128)(2,1)} copy-done((bf16[32,8,4096]{2,1,0:T(8,128)(2,1)}, bf16[32,8,4096]{2,1,0:T(8,128)(2,1)S(1)}, u32[]{:S(2)}) %copy-start) | copy-done | bytes 2097176
  30.9 5.2 %legendre.1 = f32[2,32,2,2048]{3,2,1,0:T(2,128)} custom-call(s32[2]{0:T(128)} %pad_add_fusion.where, f32[2,8,16,128]{3,2,1,0:T(8,128)} %bitcast.11, f32[4,4]{1,0:T(4,128)} %weight.1, bf16[32,8,4096]{2,1,0:T(8,128)(2,1)} %own.1, bf16[32,8,4096]{2,1,0:T(8,128)(2,1)} %copy-done), custom_call_target="tpu_custom_call" | custom-call | tf_op jit(solution)/shard_map/legendre/pallas_call | solution.py:190
Async XLA Ops:
  0.0 29.6 %collective-permute-start = (bf16[32,8,4096]{2,1,0:T(8,128)(2,1)}, bf16[32,8,4096]{2,1,0:T(8,128)(2,1)S(1)}, u32[]{:S(2)}, u32[]{:S(2)}) collective-permute-start(bf16[32,8,4096]{2,1,0:T(8,128)(2,1)} %own.1), channel_id=1, source_target_pairs={{0,1},{1,0},{2,3},{3,2},{4,5},{5,4},{6,7},{7,6},{8,9},{9,8},{10,11... | collective-permute-start | bytes 6291464 | tf_op jit(solution)/shard_map/ppermute | solution.py:159
  14.0 14.9 %all-to-all-start = ((f32[16,16,128]{2,1,0:T(8,128)}), f32[16,16,128]{2,1,0:T(8,128)S(1)}, u32[]{:S(2)}, u32[]{:S(2)}) async-start(f32[16,16,128]{2,1,0:T(8,128)} %bitcast.4), calls=%async_computation | async-start | bytes 262144 | tf_op jit(solution)/shard_map/all_to_all | solution.py:181
  29.6 1.3 %copy-start = (bf16[32,8,4096]{2,1,0:T(8,128)(2,1)}, bf16[32,8,4096]{2,1,0:T(8,128)(2,1)S(1)}, u32[]{:S(2)}) copy-start(bf16[32,8,4096]{2,1,0:T(8,128)(2,1)S(1)} %collective-permute-done.other) | copy-start | bytes 6291460

commit v2 on v1

v2 whole, which is shorter than its diff:
```python
import functools
import math

import jax
import jax.numpy as jnp
import numpy as np
from jax import lax
from jax.experimental import pallas as pl
from jax.experimental.pallas import tpu as pltpu
from jax.sharding import PartitionSpec as P

NP = 8192
M = 128
TP = 128
CYCLE_DEV = 2
SHELL_DEV = 2

f32 = jnp.float32
bf16 = jnp.bfloat16


def split(x):
    high = x.astype(bf16)
    return high, (x - high.astype(f32)).astype(bf16)


def dot(a, b, contract=((1,), (0,))):
    return lax.dot_general(a, b, (contract, ((), ())), preferred_element_type=f32)


def split_np(x):
    high = x.astype(np.float32).astype(bf16)
    return np.stack([high, (x - high.astype(np.float64)).astype(np.float32).astype(bf16)])


@functools.cache
def tables():
    order = np.arange(M)
    pixel = np.arange(TP)
    spread = np.exp(-((pixel[:, None] - pixel[None, :]) ** 2) / 18.0)
    angle = (order[:, None] * pixel[None, :] % NP) * (2.0 * math.pi / NP)
    modes = split_np(np.concatenate([np.cos(angle), -np.sin(angle)], 0) @ spread)
    place = np.arange(NP // TP)
    turn = (order[:, None] * place[None, :] * TP % NP) * (2.0 * math.pi / NP)
    phase = split_np(np.concatenate([np.cos(turn), -np.sin(turn)], 0))
    return modes, phase


HIGH = 8
LOW = TP // HIGH


def histogram(cyc, pix, mass, start):
    count = cyc.shape[-1]
    faint = math.exp(-0.5)
    level = lax.broadcasted_iota(jnp.int32, (LOW, count), 0)
    lane = lax.broadcasted_iota(jnp.int32, (LOW, TP), 1)
    slot, tile = lane // 16, lane % 8
    none = jnp.zeros((16, count), bf16)
    sums = [jnp.zeros((LOW, TP), f32) for _ in range(HIGH)]
    for g in range(8):
        at = pl.ds(pl.multiple_of(start + g * 8, 8), 8)
        c8, x8, m8 = cyc[0, at, :], pix[0, at, :], mass[0, at, :]
        far = m8 * faint
        near = jnp.concatenate([jnp.where(c8 == 0, m8, far), jnp.where(c8 == 0, far, m8)], 0)
        pieces = split(near)
        top = x8 // LOW
        top = jnp.concatenate([top, top], 0).astype(jnp.int16)
        masks = [top == ((s - g) % HIGH) for s in range(8)]
        right = jnp.concatenate([jnp.where(k, p, none) for p in pieces for k in masks], 0)
        low = x8 % LOW
        left = [jnp.where(level == low[j : j + 1, :], 1.0, 0.0).astype(bf16) for j in range(8)]
        got = dot(jnp.concatenate(left, 0), right, ((1,), (1,)))
        got = got[:, :TP] + got[:, TP:]
        mine = got[:LOW]
        for j in range(1, 8):
            mine = jnp.where(tile == j, got[j * LOW : (j + 1) * LOW], mine)
        for s in range(8):
            e = (s - g) % HIGH
            sums[e] = jnp.where(slot == s, mine, sums[e])
    sums = [sums[0]] + [pltpu.roll(sums[e], TP - 16 * e, 1) for e in range(1, HIGH)]
    return jnp.concatenate(sums, 0)


def deposit_kernel(
    cyc_at, pix_at, mass_at, place_at, shell_at, block_at, modes_at, phase_at, basis, out, own,
    cyc, pix, mass, place, shell, block, modes_tab, phase_tab, h, phase, rot, row_sems, sems, *, blocks,
):
    tiles = cyc.shape[1]
    wide = CYCLE_DEV * tiles
    bins = SHELL_DEV * blocks
    parts = tiles // 64
    me = lax.axis_index("sky")

    def rows(part):
        at = pl.ds(part * 64, 64)
        pairs = ((cyc_at, cyc), (pix_at, pix), (mass_at, mass))
        return [
            pltpu.make_async_copy(a.at[:, at, :], b.at[:, at, :], row_sems.at[part, i])
            for i, (a, b) in enumerate(pairs)
        ]

    degrees = own.shape[2]
    near = pl.ds(pl.multiple_of(lax.axis_index("sub") * degrees, 128), degrees)
    pairs = ((place_at, place), (shell_at, shell), (block_at, block), (phase_at, phase_tab), (modes_at, modes_tab))
    pairs += ((basis.at[:, :, near], own),)
    small = [pltpu.make_async_copy(a, b, sems.at[i]) for i, (a, b) in enumerate(pairs)]
    for copy in small[:4] + [c for part in range(parts) for c in rows(part)] + small[4:]:
        copy.start()

    for copy in small[:4]:
        copy.wait()
    column = lax.broadcasted_iota(jnp.int32, (tiles, wide), 1)
    double = (column // 16) * 8 + column % 8 == lax.broadcasted_iota(jnp.int32, (tiles, wide), 0)
    double = jnp.where(double, 1.0, 0.0).astype(bf16)
    marks = jnp.concatenate([place[...], shell[...] * blocks + block[...]], 0)
    named = dot(marks.astype(f32).astype(bf16), double).astype(jnp.int32)
    places = phase_tab.shape[2]
    hot_place = lax.broadcasted_iota(jnp.int32, (places, wide), 0) == named[0:1]
    hot_place = jnp.where(hot_place, 1.0, 0.0).astype(bf16)
    phase[...] = dot(phase_tab[0], hot_place) + dot(phase_tab[1], hot_place)
    column = lax.broadcasted_iota(jnp.int32, (1, wide), 1)
    key = (column // 8 % CYCLE_DEV) * bins + named[1:2]
    hot_bin = lax.broadcasted_iota(jnp.int32, (CYCLE_DEV * bins, wide), 0) == key
    hot_bin = jnp.where(hot_bin, 1.0, 0.0).astype(bf16)

    for part in range(parts):
        for copy in rows(part):
            copy.wait()
        h[:, part * TP : (part + 1) * TP] = histogram(cyc, pix, mass, part * 64)

    small[4].wait()
    high, low = split(h[...])
    modes = dot(modes_tab[0], high) + dot(modes_tab[1], high) + dot(modes_tab[0], low)
    real, imag, cosine, sine = modes[:M], modes[M:], phase[:M, :], phase[M:, :]
    turned = real * cosine - imag * sine, real * sine + imag * cosine
    sums = jnp.zeros((CYCLE_DEV * bins, 2 * M), f32)
    for i in range(wide // TP):
        for j in range(2):
            rot[i, pl.ds(j, M, 2), :] = turned[j][:, i * TP : (i + 1) * TP]
    for i in range(wide // TP):
        left = hot_bin[:, i * TP : (i + 1) * TP]
        for piece in split(rot[i]):
            sums = sums + dot(left, piece, ((1,), (1,)))
    width = out.shape[-1] // CYCLE_DEV
    for z in range(out.shape[0]):
        out[me ^ z] = jnp.concatenate(
            [sums[k * bins : (k + 1) * bins, z * width : (z + 1) * width] for k in range(CYCLE_DEV)], 1
        )
    small[5].wait()


LIMIT = 24 << 20


def stages_of(sky, shells):
    bits = [("sub", 1)]
    bits += [("sky", 1 << i) for i in range(sky.bit_length() - 1)]
    bits += [("shell", 1 << i) for i in range(shells.bit_length() - 1)]
    return [[bit] for bit in bits]


AXES = ("sky", "shell", "sub")


def swap(x, change):
    sizes = [lax.axis_size(a) for a in AXES]
    pairs = []
    for here in np.ndindex(*sizes):
        there = [i ^ change.get(a, 0) for a, i in zip(AXES, here)]
        pairs.append((int(np.ravel_multi_index(here, sizes)), int(np.ravel_multi_index(there, sizes))))
    return lax.ppermute(x, AXES, pairs)


def exchange(y, stages):
    groups = {0: y}
    for number, steps in enumerate(stages):
        last = number == len(stages) - 1
        skies = [bit for axis, bit in steps if axis == "sky"]
        width = len(skies)
        fresh = {}
        for g, value in groups.items():
            rest = value.shape[1:]
            value = value.reshape((-1,) + (2,) * width + rest)
            for chosen in range(1 << len(steps)):
                change, index, target = {}, [slice(None)] + [0] * width, g
                for i, (axis, bit) in enumerate(steps):
                    if chosen >> i & 1:
                        change[axis] = change.get(axis, 0) ^ bit
                        if axis == "sky":
                            index[width - skies.index(bit)] = 1
                        if axis == "shell":
                            target ^= bit
                piece = value[tuple(index)]
                fresh.setdefault(target, []).append(swap(piece, change) if change else piece)
        if last:
            return [fresh[g] for g in sorted(fresh)]
        groups = {g: sum(pieces[1:], pieces[0]) for g, pieces in fresh.items()}


def legendre_kernel(weight, own, other, *refs, counts, blocks):
    refs, out, left = refs[:-2], refs[-2], refs[-1]
    lanes = refs[0].shape[-1]
    orders = own.shape[0]
    cycles = own.shape[1]
    width = orders * cycles
    half = lanes // CYCLE_DEV
    planes = out.shape[0]
    sub, place = lax.axis_index("sub"), lax.axis_index("shell")

    @pl.when(pl.program_id(0) == 0)
    def _():
        first = place * planes
        maps = []
        for x, count in enumerate(counts):
            at = sum(counts[:x])
            total = refs[at][0]
            for i in range(1, count):
                total = total + refs[at + i][0]
            total = (total * (2.0 * math.pi / NP)).astype(bf16).astype(f32)
            maps += [
                ((place ^ x) * SHELL_DEV + s, total[s * blocks : (s + 1) * blocks])
                for s in range(SHELL_DEV)
            ]
        column = lax.broadcasted_iota(jnp.int32, (blocks, width), 1)
        row = lax.broadcasted_iota(jnp.int32, (blocks, width), 0)
        wide = lax.broadcasted_iota(jnp.int32, (half, width), 1)
        keep = lax.broadcasted_iota(jnp.int32, (half, width), 0) // 2 == wide // cycles
        even = wide % CYCLE_DEV == 0
        for side in range(2):
            mine = sub if side == 0 else 1 - sub
            cycle = mine * cycles + column % cycles
            spread = jnp.where(row == cycle // CYCLE_DEV, 1.0, 0.0).astype(bf16)
            for i in range(planes):
                total = jnp.zeros((blocks, lanes), f32)
                for s, value in maps:
                    factor = jnp.where(s <= first + i, weight[first + i, s], 0.0)
                    total = total + factor * value
                high, low = split(total)
                for j, piece in enumerate((high, low)):
                    grown = dot(piece, spread, ((0,), (0,)))
                    grown = jnp.where(even, grown[:half], grown[half:])
                    grown = jnp.where(keep, grown, 0.0).astype(bf16)
                    start = (j * planes + i) * half
                    left[side, start : start + half, :] = grown

    span = out.shape[-1]
    start = pl.program_id(0) * span
    a = own[:, :, pl.ds(pl.multiple_of(start, 128), span)].reshape(width, span)
    start = start + sub * own.shape[2]
    b = other[:, :, pl.ds(pl.multiple_of(start, 128), span)].reshape(width, span)
    result = dot(left[0], a) + dot(left[1], b)
    result = result[: planes * half] + result[planes * half :]
    for i in range(planes):
        for m in range(orders):
            start = i * half + m * 2
            out[i, m, :, :] = result[start : start + 2, :]


def body(part_cycle, part_pixel, part_mass, tile_block, tile_shell, tile_pixel, basis, lens_weight):
    sky, sub, shells = lax.axis_size("sky"), lax.axis_size("sub"), lax.axis_size("shell")
    tiles, count = part_cycle.shape[1:]
    orders, cycles, degrees = basis.shape
    blocks = cycles * sub // CYCLE_DEV
    sources = lens_weight.shape[0] // shells
    modes_tab, phase_tab = (jnp.asarray(t) for t in tables())

    other = lax.ppermute(basis, "sub", [(i, (i + 1) % sub) for i in range(sub)])

    lanes = CYCLE_DEV * orders * 2
    bins = SHELL_DEV * blocks
    own_degrees = degrees // sub
    anywhere = pl.BlockSpec(memory_space=pltpu.HBM)
    vmem = pl.BlockSpec(memory_space=pltpu.VMEM)
    send, own = pl.pallas_call(
        functools.partial(deposit_kernel, blocks=blocks),
        out_shape=(
            jax.ShapeDtypeStruct((sky, bins, lanes), f32),
            jax.ShapeDtypeStruct((orders, cycles, own_degrees), bf16),
        ),
        in_specs=[anywhere] * 9,
        out_specs=(vmem, vmem),
        scratch_shapes=[
            pltpu.VMEM((1, tiles, count), jnp.int32),
            pltpu.VMEM((1, tiles, count), jnp.int32),
            pltpu.VMEM((1, tiles, count), f32),
            pltpu.VMEM((1, tiles), jnp.int32),
            pltpu.VMEM((1, tiles), jnp.int32),
            pltpu.VMEM((1, tiles), jnp.int32),
            pltpu.VMEM(modes_tab.shape, bf16),
            pltpu.VMEM(phase_tab.shape, bf16),
            pltpu.VMEM((TP, CYCLE_DEV * tiles), f32),
            pltpu.VMEM((2 * M, CYCLE_DEV * tiles), f32),
            pltpu.VMEM((CYCLE_DEV * tiles // TP, 2 * M, TP), f32),
            pltpu.SemaphoreType.DMA((tiles // 64, 3)),
            pltpu.SemaphoreType.DMA((6,)),
        ],
        compiler_params=pltpu.CompilerParams(vmem_limit_bytes=LIMIT),
        name="deposit",
    )(
        *(
            pltpu.with_memory_space_constraint(x, pltpu.HBM)
            for x in (
                part_cycle,
                part_pixel,
                part_mass,
                tile_pixel,
                tile_shell,
                tile_block.reshape(1, tiles),
                modes_tab,
                phase_tab,
                basis,
            )
        )
    )
    parts = exchange(send, stages_of(sky, shells))

    span = min(own_degrees, 512)
    half = orders * 2
    flat = [piece for group in parts for piece in group]
    return pl.pallas_call(
        functools.partial(legendre_kernel, counts=[len(group) for group in parts], blocks=blocks),
        out_shape=jax.ShapeDtypeStruct((sources, orders, 2, own_degrees), f32),
        grid=(own_degrees // span,),
        in_specs=[pl.BlockSpec(memory_space=pltpu.SMEM), vmem, vmem] + [vmem] * len(flat),
        out_specs=pl.BlockSpec((sources, orders, 2, span), lambda j: (0, 0, 0, j)),
        scratch_shapes=[pltpu.VMEM((2, 2 * sources * half, orders * cycles), bf16)],
        compiler_params=pltpu.CompilerParams(vmem_limit_bytes=LIMIT),
        name="legendre",
    )(lens_weight, own, other, *flat)


def solution(mesh):
    return jax.shard_map(
        body,
        mesh=mesh,
        in_specs=(
            P("shell", ("sky", "sub"), None),
            P("shell", ("sky", "sub"), None),
            P("shell", ("sky", "sub"), None),
            P("shell", ("sky", "sub"), None),
            P("shell", ("sky", "sub")),
            P("shell", ("sky", "sub")),
            P("sky", "sub", None),
            P(),
        ),
        out_specs=P(("groups", "shell"), "sky", None, "sub"),
        check_vma=False,
    )
```

time: 36.5 us -> 23.1 us (0.63)
  Pallas kernels: 17.1 us -> 8.33 us
  local copies, waits for them, and re-layouts: 3.66 us -> 0.01 us
  waiting for transfers between devices: 7.25 us -> 6.37 us
  starting transfers between devices: 7.48 us -> 8.22 us
  other arithmetic: 0.65 us -> 0.01 us
    ppermute x0 -> x4, starting transfers between devices: none -> 7.73 us  [swap(): return lax.ppermute(x, AXES, pairs)]
    all_to_all x1 -> x0, waiting for transfers between devices: 7.25 us -> none  [body(): recv = lax.all_to_all(send, ('sky', 'shell', 'sub'), 0, 0, tiled=True)]
    all_to_all x1 -> x0, starting transfers between devices: 6.99 us -> none  [body(): recv = lax.all_to_all(send, ('sky', 'shell', 'sub'), 0, 0, tiled=True)]
    pallas_call x1, Pallas kernels: 11.9 us -> 4.98 us  [body(): pl.pallas_call(functools.partial(deposit_kernel, blocks=blocks), out_shap...]
    ppermute x0 -> x4, waiting for transfers between devices: none -> 6.36 us  [swap(): return lax.ppermute(x, AXES, pairs)]
    pallas_call x1, Pallas kernels: 5.22 us -> 3.35 us  [body(): pl.pallas_call(functools.partial(legendre_kernel, counts=[len(group) for...]
    unnamed x2, local copies, waits for them, and re-layouts: 1.33 us -> 0.01 us
    reshape x2 -> x0, local copies, waits for them, and re-layouts: 0.9 us -> none  [body(): binned.reshape(CYCLE_DEV, SHELL_DEV * blocks, sky, orders * 2)]
  transfers between devices with their start and end apart: 2 -> 5, of which waited for: 1 -> 4; matrix products, arithmetic and copies ran while one was open for 8% -> 0% of each run, Pallas kernels for 33% -> 22%
where the time goes in v2:
time: 23.1 us; the launch traced here: 23 us
  Pallas kernels  8.33 us (36%)
  starting transfers between devices  8.22 us (36%)
  waiting for transfers between devices  6.37 us (28%)
    ppermute x4, starting transfers between devices, swap(): return lax.ppermute(x, AXES, pairs)  7.73 us
    ppermute x4, waiting for transfers between devices, swap(): return lax.ppermute(x, AXES, pairs)  6.36 us
    pallas_call x1, Pallas kernels, body(): pl.pallas_call(functools.partial(deposit_kernel, blocks=blocks), out_shap...  4.98 us
    pallas_call x1, Pallas kernels, body(): pl.pallas_call(functools.partial(legendre_kernel, counts=[len(group) for...  3.35 us
    ppermute x1, starting transfers between devices, body(): other = lax.ppermute(basis, 'sub', [(i, (i + 1) % sub) for i in range(sub)])  0.49 us
  transfers between devices with their start and end apart: 5, of which 4 were waited for; matrix products, arithmetic and copies ran while one was open for 0% of the time, Pallas kernels for 22%

profile of v2, /device:TPU:0, one launch (start us, length us, event | category | flops | bytes accessed | tf_op | source)
XLA Modules:
  0.0 23.0 jit_solution(4228178513593860474)
XLA Ops:
  0.0 0.0 copy-start
  0.0 0.5 %collective-permute-start = (bf16[32,8,4096]{2,1,0:T(8,128)(2,1)}, bf16[32,8,4096]{2,1,0:T(8,128)(2,1)S(1)}, u32[]{:S(2)}, u32[]{:S(2)}) collective-permute-start(bf16[32,8,4096]{2,1,0:T(8,128)(2,1)} %basis.1), channel_id=1, source_target_pairs={{0,1},{1,0},{2,3},{3,2},{4,5},{5,4},{6,7},{7,6},{8,9},{9,8},{10,11... | collective-permute-start | bytes 6291464 | tf_op jit(solution)/shard_map/ppermute | solution.py:268
  0.5 5.0 %deposit.1 = (f32[4,16,128]{2,1,0:T(8,128)S(1)}, bf16[32,8,2048]{2,1,0:T(8,128)(2,1)S(1)}) custom-call(s32[1,256,256]{2,1,0:T(8,128)} %cyc_at.1, s32[1,256,256]{2,1,0:T(8,128)} %pix_at.1, f32[1,256,256]{2,1,0:T(8,128)} %mass_at.1, s32[1,256]{1,0:T(1,128)} %place_at.1, s32[1,256]{1,0:T(1,128)} %shell_at.1, s32[1,256]{1,0:T(1,128)} %bitcast.24, ...), custom_call_target="tpu_custom_call" | custom-call | tf_op jit(solution)/shard_map/deposit/pallas_call | solution.py:275
  5.5 0.1 collective-permute-start.1
  5.6 1.2 %collective-permute-done.1 = f32[4,16,128]{2,1,0:T(8,128)S(1)} collective-permute-done((f32[4,16,128]{2,1,0:T(8,128)S(1)}, f32[4,16,128]{2,1,0:T(8,128)S(1)}, u32[]{:S(2)}, u32[]{:S(2)}) %collective-permute-start.1) | collective-permute-done | bytes 32800 | tf_op jit(solution)/shard_map/ppermute | solution.py:172
  6.8 2.8 %collective-permute-start.2 = (f32[2,16,128]{2,1,0:T(8,128)S(1)}, f32[2,16,128]{2,1,0:T(8,128)S(1)}, u32[]{:S(2)}, u32[]{:S(2)}) collective-permute-start(f32[2,16,128]{2,1,0:T(8,128)S(1)} %slice_bitcast_fusion), channel_id=1, source_target_pairs={{0,4},{1,5},{2,6},{3,7},{4,0},{5,1},{6,2},{7,3},{8,12},{9,13},{10,... | collective-permute-start | bytes 49160 | tf_op jit(solution)/shard_map/ppermute | solution.py:172
  9.6 1.7 %collective-permute-done.2 = f32[2,16,128]{2,1,0:T(8,128)S(1)} collective-permute-done((f32[2,16,128]{2,1,0:T(8,128)S(1)}, f32[2,16,128]{2,1,0:T(8,128)S(1)}, u32[]{:S(2)}, u32[]{:S(2)}) %collective-permute-start.2) | collective-permute-done | bytes 16416 | tf_op jit(solution)/shard_map/ppermute | solution.py:172
  11.3 3.0 %collective-permute-start.3 = (f32[1,16,128]{2,1,0:T(8,128)S(1)}, f32[1,16,128]{2,1,0:T(8,128)S(1)}, u32[]{:S(2)}, u32[]{:S(2)}) collective-permute-start(f32[1,16,128]{2,1,0:T(8,128)S(1)} %slice_bitcast_fusion.2), channel_id=1, source_target_pairs={{0,8},{1,9},{2,10},{3,11},{4,12},{5,13},{6,14},{7,15},{8,0},{9,1},... | collective-permute-start | bytes 24584 | tf_op jit(solution)/shard_map/ppermute | solution.py:172
  14.3 1.6 %collective-permute-done.3 = f32[1,16,128]{2,1,0:T(8,128)S(1)} collective-permute-done((f32[1,16,128]{2,1,0:T(8,128)S(1)}, f32[1,16,128]{2,1,0:T(8,128)S(1)}, u32[]{:S(2)}, u32[]{:S(2)}) %collective-permute-start.3) | collective-permute-done | bytes 8224 | tf_op jit(solution)/shard_map/ppermute | solution.py:172
  16.0 1.8 %collective-permute-start.4 = (f32[1,16,128]{2,1,0:T(8,128)S(1)}, f32[1,16,128]{2,1,0:T(8,128)S(1)}, u32[]{:S(2)}, u32[]{:S(2)}) collective-permute-start(f32[1,16,128]{2,1,0:T(8,128)S(1)} %fusion.2.refs_0_), channel_id=1, source_target_pairs={{0,2},{1,3},{2,0},{3,1},{4,6},{5,7},{6,4},{7,5},{8,10},{9,11},{10,... | collective-permute-start | bytes 24584 | tf_op jit(solution)/shard_map/ppermute | solution.py:172
  17.8 1.8 %collective-permute-done.4.refs_1_ = f32[1,16,128]{2,1,0:T(8,128)S(1)} collective-permute-done((f32[1,16,128]{2,1,0:T(8,128)S(1)}, f32[1,16,128]{2,1,0:T(8,128)S(1)}, u32[]{:S(2)}, u32[]{:S(2)}) %collective-permute-start.4) | collective-permute-done | bytes 8224 | tf_op jit(solution)/shard_map/ppermute | solution.py:172
  19.6 0.0 collective-permute-done.other
  19.6 0.0 copy-done
  19.6 3.4 %legendre.1 = f32[2,32,2,2048]{3,2,1,0:T(2,128)} custom-call(f32[4,4]{1,0:T(4,128)S(1)} %copy-done, bf16[32,8,2048]{2,1,0:T(8,128)(2,1)S(1)} %get-tuple-element.7.own, bf16[32,8,4096]{2,1,0:T(8,128)(2,1)S(1)} %collective-permute-done.other, f32[1,16,128]{2,1,0:T(8,128)S(1)} %fusion.2.refs_0_, f32[1,16,128]{2,1,0:T(8,128)S(1)} %collective-permute-done.4.refs_1_), custom_call_target="tpu_custom_call" | custom-call | tf_op jit(solution)/shard_map/legendre/pallas_call | solution.py:321
  (5 shorter events, 0.0 us)
Async XLA Ops:
  0.0 19.6 %copy-start = (f32[4,4]{1,0:T(4,128)S(1)}, f32[4,4]{1,0:T(4,128)}, u32[]{:S(2)}) copy-start(f32[4,4]{1,0:T(4,128)} %weight.1) | copy-start | bytes 196
  0.0 19.6 %collective-permute-start = (bf16[32,8,4096]{2,1,0:T(8,128)(2,1)}, bf16[32,8,4096]{2,1,0:T(8,128)(2,1)S(1)}, u32[]{:S(2)}, u32[]{:S(2)}) collective-permute-start(bf16[32,8,4096]{2,1,0:T(8,128)(2,1)} %basis.1), channel_id=1, source_target_pairs={{0,1},{1,0},{2,3},{3,2},{4,5},{5,4},{6,7},{7,6},{8,9},{9,8},{10,11... | collective-permute-start | bytes 6291464 | tf_op jit(solution)/shard_map/ppermute | solution.py:268
  5.5 1.3 %collective-permute-start.1 = (f32[4,16,128]{2,1,0:T(8,128)S(1)}, f32[4,16,128]{2,1,0:T(8,128)S(1)}, u32[]{:S(2)}, u32[]{:S(2)}) collective-permute-start(f32[4,16,128]{2,1,0:T(8,128)S(1)} %get-tuple-element.8), channel_id=1, source_target_pairs={{0,1},{1,0},{2,3},{3,2},{4,5},{5,4},{6,7},{7,6},{8,9},{9,8},{10,11... | collective-permute-start | bytes 98312 | tf_op jit(solution)/shard_map/ppermute | solution.py:172
  6.8 4.5 %collective-permute-start.2 = (f32[2,16,128]{2,1,0:T(8,128)S(1)}, f32[2,16,128]{2,1,0:T(8,128)S(1)}, u32[]{:S(2)}, u32[]{:S(2)}) collective-permute-start(f32[2,16,128]{2,1,0:T(8,128)S(1)} %slice_bitcast_fusion), channel_id=1, source_target_pairs={{0,4},{1,5},{2,6},{3,7},{4,0},{5,1},{6,2},{7,3},{8,12},{9,13},{10,... | collective-permute-start | bytes 49160 | tf_op jit(solution)/shard_map/ppermute | solution.py:172
  11.3 4.7 %collective-permute-start.3 = (f32[1,16,128]{2,1,0:T(8,128)S(1)}, f32[1,16,128]{2,1,0:T(8,128)S(1)}, u32[]{:S(2)}, u32[]{:S(2)}) collective-permute-start(f32[1,16,128]{2,1,0:T(8,128)S(1)} %slice_bitcast_fusion.2), channel_id=1, source_target_pairs={{0,8},{1,9},{2,10},{3,11},{4,12},{5,13},{6,14},{7,15},{8,0},{9,1},... | collective-permute-start | bytes 24584 | tf_op jit(solution)/shard_map/ppermute | solution.py:172
  16.0 3.7 %collective-permute-start.4 = (f32[1,16,128]{2,1,0:T(8,128)S(1)}, f32[1,16,128]{2,1,0:T(8,128)S(1)}, u32[]{:S(2)}, u32[]{:S(2)}) collective-permute-start(f32[1,16,128]{2,1,0:T(8,128)S(1)} %fusion.2.refs_0_), channel_id=1, source_target_pairs={{0,2},{1,3},{2,0},{3,1},{4,6},{5,7},{6,4},{7,5},{8,10},{9,11},{10,... | collective-permute-start | bytes 24584 | tf_op jit(solution)/shard_map/ppermute | solution.py:172

commit v3 on v2

v3 whole, which is shorter than its diff:
```python
import functools
import math

import jax
import jax.numpy as jnp
import numpy as np
from jax import lax
from jax.experimental import pallas as pl
from jax.experimental.pallas import tpu as pltpu
from jax.sharding import PartitionSpec as P

NP = 8192
M = 128
TP = 128
CYCLE_DEV = 2
SHELL_DEV = 2

f32 = jnp.float32
bf16 = jnp.bfloat16


def split(x):
    high = x.astype(bf16)
    return high, (x - high.astype(f32)).astype(bf16)


def dot(a, b, contract=((1,), (0,))):
    return lax.dot_general(a, b, (contract, ((), ())), preferred_element_type=f32)


def split_np(x):
    high = x.astype(np.float32).astype(bf16)
    return np.concatenate([high, (x - high.astype(np.float64)).astype(np.float32).astype(bf16)], 1)


@functools.cache
def tables():
    order = np.arange(M)
    pixel = np.arange(TP)
    spread = np.exp(-((pixel[:, None] - pixel[None, :]) ** 2) / 18.0)
    angle = (order[:, None] * pixel[None, :] % NP) * (2.0 * math.pi / NP)
    modes = split_np(np.concatenate([np.cos(angle), -np.sin(angle)], 0) @ spread)
    place = np.arange(NP // TP)
    turn = (order[:, None] * place[None, :] * TP % NP) * (2.0 * math.pi / NP)
    phase = split_np(np.concatenate([np.cos(turn), -np.sin(turn)], 0))
    return modes, phase


HIGH = 8
LOW = TP // HIGH
GROUP = 4
SHIFT = LOW.bit_length() - 1


def histogram(cyc, pix, mass, start):
    count = cyc.shape[-1]
    level = lax.broadcasted_iota(jnp.int16, (LOW, count), 0)
    lane = lax.broadcasted_iota(jnp.int32, (LOW, TP), 1)
    slot, tile = lane >> 4, lane & 7
    one, none = jnp.ones((LOW, count), bf16), jnp.zeros((16, count), bf16)
    sums = [jnp.zeros((LOW, TP), f32) for _ in range(HIGH)]
    for g in range(8):
        at = pl.ds(start + g * 8, 8)
        c8, x8, m8 = cyc[0, at, :], pix[0, at, :], mass[0, at, :]
        top = x8 >> SHIFT
        first = jnp.where(c8 == 0, top, HIGH)
        other = jnp.where(c8 == 0, HIGH, top)
        top = jnp.concatenate([first, other], 0).astype(jnp.int16)
        masks = [top == (s - g) % HIGH for s in range(8)]
        pieces = split(jnp.concatenate([m8, m8], 0))
        right = jnp.concatenate([jnp.where(k, p, none) for p in pieces for k in masks], 0)
        low = (x8 & (LOW - 1)).astype(jnp.int16)
        left = [jnp.where(level == low[j : j + 1, :], one, none) for j in range(8)]
        got = dot(jnp.concatenate(left, 0), right, ((1,), (1,)))
        got = got[:, :TP] + got[:, TP:]
        mine = got[:LOW]
        for j in range(1, 8):
            mine = jnp.where(tile == j, got[j * LOW : (j + 1) * LOW], mine)
        for s in range(8):
            e = (s - g) % HIGH
            sums[e] = jnp.where(slot == s, mine, sums[e])
    sums = [sums[0]] + [pltpu.roll(sums[e], TP - 16 * e, 1) for e in range(1, HIGH)]
    return jnp.concatenate(sums, 0)


def deposit_kernel(
    cyc_at, pix_at, mass_at, place_at, shell_at, block_at, modes_at, phase_at, basis, out, own,
    cyc, pix, mass, place, shell, block, modes_tab, phase_tab, rot, row_sems, sems, *, blocks,
):
    tiles = cyc.shape[1]
    wide = CYCLE_DEV * tiles
    bins = SHELL_DEV * blocks
    parts = tiles // 64
    me = lax.axis_index("sky")

    def rows(part):
        at = pl.ds(part * 64, 64)
        pairs = ((cyc_at, cyc), (pix_at, pix), (mass_at, mass))
        return [
            pltpu.make_async_copy(a.at[:, at, :], b.at[:, at, :], row_sems.at[part, i])
            for i, (a, b) in enumerate(pairs)
        ]

    degrees = own.shape[2]
    near = pl.ds(pl.multiple_of(lax.axis_index("sub") * degrees, 128), degrees)
    pairs = ((place_at, place), (shell_at, shell), (block_at, block), (phase_at, phase_tab), (modes_at, modes_tab))
    pairs += ((basis.at[:, :, near], own),)
    small = [pltpu.make_async_copy(a, b, sems.at[i]) for i, (a, b) in enumerate(pairs)]
    for copy in [c for part in range(parts) for c in rows(part)] + small:
        copy.start()

    for copy in [c for part in range(parts) for c in rows(part)] + small[:5]:
        copy.wait()
    column = lax.broadcasted_iota(jnp.int32, (64, TP), 1)
    double = ((column >> 4) << 3) + (column & 7) == lax.broadcasted_iota(jnp.int32, (64, TP), 0)
    double = jnp.where(double, 1.0, 0.0).astype(bf16)
    marks = jnp.concatenate([place[...], shell[...] * blocks + block[...]], 0).astype(f32).astype(bf16)
    named = [dot(marks[:, part * 64 : (part + 1) * 64], double) for part in range(parts)]
    named = jnp.concatenate(named, 1).astype(jnp.int32)
    places = phase_tab.shape[1] // 2
    hot_place = lax.broadcasted_iota(jnp.int32, (places, wide), 0) == named[0:1]
    hot_place = jnp.where(hot_place, 1.0, 0.0).astype(bf16)
    column = lax.broadcasted_iota(jnp.int32, (1, wide), 1)
    key = ((column >> 3) & 1) * bins + named[1:2]
    hot_bin = lax.broadcasted_iota(jnp.int32, (CYCLE_DEV * bins, wide), 0) == key
    hot_bin = jnp.where(hot_bin, 1.0, 0.0).astype(bf16)

    sums = jnp.zeros((CYCLE_DEV * bins, 2 * M), f32)
    for part in range(0, parts, GROUP):
        at = slice(part * TP, (part + GROUP) * TP)
        h = [histogram(cyc, pix, mass, i * 64) for i in range(part, part + GROUP)]
        phase = dot(phase_tab[...], jnp.concatenate([hot_place, hot_place], 0))
        high, low = split(jnp.concatenate(h, 1))
        modes = dot(modes_tab[...], jnp.concatenate([high, high], 0)) + dot(modes_tab[:, :TP], low)
        real, imag, cosine, sine = modes[:M], modes[M:], phase[:M, at], phase[M:, at]
        turned = real * cosine - imag * sine, real * sine + imag * cosine
        for i in range(GROUP):
            for j in range(2):
                rot[part + i, pl.ds(j, M, 2), :] = turned[j][:, i * TP : (i + 1) * TP]
        pieces = [split(rot[part + i]) for i in range(GROUP)]
        for j in range(2):
            right = jnp.concatenate([p[j] for p in pieces], 1)
            sums = sums + dot(hot_bin[:, at], right, ((1,), (1,)))
    faint = math.exp(-0.5)
    sums = sums + faint * jnp.concatenate([sums[bins:], sums[:bins]], 0)
    width = out.shape[-1] // CYCLE_DEV
    for z in range(out.shape[0]):
        out[me ^ z] = jnp.concatenate(
            [sums[k * bins : (k + 1) * bins, z * width : (z + 1) * width] for k in range(CYCLE_DEV)], 1
        )
    small[5].wait()


LIMIT = 24 << 20
SPAN = 512


def stages_of(sky, shells):
    bits = [("sub", 1)]
    bits += [("sky", 1 << i) for i in range(sky.bit_length() - 1)]
    bits += [("shell", 1 << i) for i in range(shells.bit_length() - 1)]
    return [[bit] for bit in bits]


AXES = ("sky", "shell", "sub")


def swap(x, change):
    sizes = [lax.axis_size(a) for a in AXES]
    pairs = []
    for here in np.ndindex(*sizes):
        there = [i ^ change.get(a, 0) for a, i in zip(AXES, here)]
        pairs.append((int(np.ravel_multi_index(here, sizes)), int(np.ravel_multi_index(there, sizes))))
    return lax.ppermute(x, AXES, pairs)


def exchange(y, stages):
    groups = {0: y}
    for number, steps in enumerate(stages):
        last = number == len(stages) - 1
        skies = [bit for axis, bit in steps if axis == "sky"]
        width = len(skies)
        fresh = {}
        for g, value in groups.items():
            rest = value.shape[1:]
            value = value.reshape((-1,) + (2,) * width + rest)
            for chosen in range(1 << len(steps)):
                change, index, target = {}, [slice(None)] + [0] * width, g
                for i, (axis, bit) in enumerate(steps):
                    if chosen >> i & 1:
                        change[axis] = change.get(axis, 0) ^ bit
                        if axis == "sky":
                            index[width - skies.index(bit)] = 1
                        if axis == "shell":
                            target ^= bit
                piece = value[tuple(index)]
                fresh.setdefault(target, []).append(swap(piece, change) if change else piece)
        if last:
            return [fresh[g] for g in sorted(fresh)]
        groups = {g: sum(pieces[1:], pieces[0]) for g, pieces in fresh.items()}


def legendre_kernel(weight, own, other, *refs, counts, blocks):
    refs, (out, left, result, sems) = refs[:-4], refs[-4:]
    lanes = refs[0].shape[-1]
    orders = own.shape[0]
    cycles = own.shape[1]
    width = orders * cycles
    half = lanes // CYCLE_DEV
    planes = result.shape[0]
    sub, place = lax.axis_index("sub"), lax.axis_index("shell")

    first = place * planes
    maps = []
    for x, count in enumerate(counts):
        at = sum(counts[:x])
        total = refs[at][0]
        for i in range(1, count):
            total = total + refs[at + i][0]
        total = (total * (2.0 * math.pi / NP)).astype(bf16).astype(f32)
        maps += [
            ((place ^ x) * SHELL_DEV + s, total[s * blocks : (s + 1) * blocks])
            for s in range(SHELL_DEV)
        ]
    column = lax.broadcasted_iota(jnp.int32, (blocks, width), 1)
    row = lax.broadcasted_iota(jnp.int32, (blocks, width), 0)
    wide = lax.broadcasted_iota(jnp.int32, (half, width), 1)
    keep = lax.broadcasted_iota(jnp.int32, (half, width), 0) // 2 == wide // cycles
    even = wide % CYCLE_DEV == 0
    for side in range(2):
        mine = sub if side == 0 else 1 - sub
        cycle = mine * cycles + column % cycles
        spread = jnp.where(row == cycle // CYCLE_DEV, 1.0, 0.0).astype(bf16)
        for i in range(planes):
            total = jnp.zeros((blocks, lanes), f32)
            for s, value in maps:
                factor = jnp.where(s <= first + i, weight[first + i, s], 0.0)
                total = total + factor * value
            high, low = split(total)
            for j, piece in enumerate((high, low)):
                grown = dot(piece, spread, ((0,), (0,)))
                grown = jnp.where(even, grown[:half], grown[half:])
                grown = jnp.where(keep, grown, 0.0).astype(bf16)
                start = (j * planes + i) * half
                left[side, start : start + half, :] = grown

    copies = []
    for step in range(own.shape[2] // SPAN):
        at = pl.ds(step * SPAN, SPAN)
        far = pl.ds(pl.multiple_of(sub * own.shape[2] + step * SPAN, 128), SPAN)
        a = own[:, :, at].reshape(width, SPAN)
        b = other[:, :, far].reshape(width, SPAN)
        value = dot(left[0], a) + dot(left[1], b)
        value = value[: planes * half] + value[planes * half :]
        for i in range(planes):
            for m in range(orders):
                start = i * half + m * 2
                result[i, m, :, at] = value[start : start + 2, :]
        copies.append(pltpu.make_async_copy(result.at[:, :, :, at], out.at[:, :, :, at], sems.at[step]))
        copies[-1].start()
    for copy in copies:
        copy.wait()


def deposit_call(part_cycle, part_pixel, part_mass, place, shell, block, basis, sky, blocks, own_degrees):
    tiles, count = part_cycle.shape[1:]
    orders, cycles, _ = basis.shape
    lanes = CYCLE_DEV * orders * 2
    bins = SHELL_DEV * blocks
    modes_tab, phase_tab = (jnp.asarray(t) for t in tables())
    anywhere = pl.BlockSpec(memory_space=pltpu.HBM)
    vmem = pl.BlockSpec(memory_space=pltpu.VMEM)
    return pl.pallas_call(
        functools.partial(deposit_kernel, blocks=blocks),
        out_shape=(
            jax.ShapeDtypeStruct((sky, bins, lanes), f32),
            jax.ShapeDtypeStruct((orders, cycles, own_degrees), bf16),
        ),
        in_specs=[anywhere] * 9,
        out_specs=(vmem, vmem),
        scratch_shapes=[
            pltpu.VMEM((1, tiles, count), jnp.int32),
            pltpu.VMEM((1, tiles, count), jnp.int32),
            pltpu.VMEM((1, tiles, count), f32),
            pltpu.VMEM((1, tiles), jnp.int32),
            pltpu.VMEM((1, tiles), jnp.int32),
            pltpu.VMEM((1, tiles), jnp.int32),
            pltpu.VMEM(modes_tab.shape, bf16),
            pltpu.VMEM(phase_tab.shape, bf16),
            pltpu.VMEM((CYCLE_DEV * tiles // TP, 2 * M, TP), f32),
            pltpu.SemaphoreType.DMA((tiles // 64, 3)),
            pltpu.SemaphoreType.DMA((6,)),
        ],
        compiler_params=pltpu.CompilerParams(vmem_limit_bytes=LIMIT),
        name="deposit",
    )(
        *(
            pltpu.with_memory_space_constraint(x, pltpu.HBM)
            for x in (
                part_cycle,
                part_pixel,
                part_mass,
                place,
                shell,
                block,
                modes_tab,
                phase_tab,
                basis,
            )
        )
    )


def legendre_call(lens_weight, own, other, parts, planes, blocks):
    orders, cycles, degrees = own.shape
    flat = [piece for group in parts for piece in group]
    vmem = pl.BlockSpec(memory_space=pltpu.VMEM)
    return pl.pallas_call(
        functools.partial(legendre_kernel, counts=[len(group) for group in parts], blocks=blocks),
        out_shape=jax.ShapeDtypeStruct((planes, orders, 2, degrees), f32),
        in_specs=[pl.BlockSpec(memory_space=pltpu.SMEM), vmem, vmem] + [vmem] * len(flat),
        out_specs=pl.BlockSpec(memory_space=pltpu.HBM),
        scratch_shapes=[
            pltpu.VMEM((2, 4 * planes * orders, orders * cycles), bf16),
            pltpu.VMEM((planes, orders, 2, degrees), f32),
            pltpu.SemaphoreType.DMA((degrees // SPAN,)),
        ],
        compiler_params=pltpu.CompilerParams(vmem_limit_bytes=LIMIT),
        name="legendre",
    )(lens_weight, own, other, *flat)


def body(part_cycle, part_pixel, part_mass, tile_block, tile_shell, tile_pixel, basis, lens_weight):
    sky, sub, shells = lax.axis_size("sky"), lax.axis_size("sub"), lax.axis_size("shell")
    tiles = part_cycle.shape[1]
    _, cycles, degrees = basis.shape
    blocks = cycles * sub // CYCLE_DEV
    other = lax.ppermute(basis, "sub", [(i, (i + 1) % sub) for i in range(sub)])
    send, own = deposit_call(
        part_cycle,
        part_pixel,
        part_mass,
        tile_pixel,
        tile_shell,
        tile_block.reshape(1, tiles),
        basis,
        sky,
        blocks,
        degrees // sub,
    )
    parts = exchange(send, stages_of(sky, shells))
    return legendre_call(lens_weight, own, other, parts, lens_weight.shape[0] // shells, blocks)


def solution(mesh):
    return jax.shard_map(
        body,
        mesh=mesh,
        in_specs=(
            P("shell", ("sky", "sub"), None),
            P("shell", ("sky", "sub"), None),
            P("shell", ("sky", "sub"), None),
            P("shell", ("sky", "sub"), None),
            P("shell", ("sky", "sub")),
            P("shell", ("sky", "sub")),
            P("sky", "sub", None),
            P(),
        ),
        out_specs=P(("groups", "shell"), "sky", None, "sub"),
        check_vma=False,
    )
```

time: 23.1 us -> 21 us (0.909)
  Pallas kernels: 8.33 us -> 6.18 us
    pallas_call x2, Pallas kernels: 8.33 us -> 6.18 us  [the longest x1 3.86 us: deposit_call(): pl.pallas_call(functools.partial(deposit_kernel, blocks=blocks), out_shap...]
  transfers between devices with their start and end apart: 5 -> 5, of which waited for: 4 -> 4; matrix products, arithmetic and copies ran while one was open for 0% -> 0% of each run, Pallas kernels for 22% -> 19%
where the time goes in v3:
time: 21 us; the launch traced here: 20.8 us
  starting transfers between devices  8.21 us (39%)
  waiting for transfers between devices  6.37 us (30%)
  Pallas kernels  6.18 us (29%)
    ppermute x4, starting transfers between devices, swap(): return lax.ppermute(x, AXES, pairs)  7.72 us
    ppermute x4, waiting for transfers between devices, swap(): return lax.ppermute(x, AXES, pairs)  6.36 us
    pallas_call x1, Pallas kernels, deposit_call(): pl.pallas_call(functools.partial(deposit_kernel, blocks=blocks), out_shap...  3.86 us
    pallas_call x1, Pallas kernels, legendre_call(): pl.pallas_call(functools.partial(legendre_kernel, counts=[len(group) for...  2.33 us
    ppermute x1, starting transfers between devices, body(): other = lax.ppermute(basis, 'sub', [(i, (i + 1) % sub) for i in range(sub)])  0.49 us
  transfers between devices with their start and end apart: 5, of which 4 were waited for; matrix products, arithmetic and copies ran while one was open for 0% of the time, Pallas kernels for 19%

profile of v3, /device:TPU:0, one launch (start us, length us, event | category | flops | bytes accessed | tf_op | source)
XLA Modules:
  0.0 20.8 jit_solution(18007035949858527214)
XLA Ops:
  0.0 0.0 copy-start
  0.0 0.5 %collective-permute-start = (bf16[32,8,4096]{2,1,0:T(8,128)(2,1)}, bf16[32,8,4096]{2,1,0:T(8,128)(2,1)S(1)}, u32[]{:S(2)}, u32[]{:S(2)}) collective-permute-start(bf16[32,8,4096]{2,1,0:T(8,128)(2,1)} %basis.1), channel_id=1, source_target_pairs={{0,1},{1,0},{2,3},{3,2},{4,5},{5,4},{6,7},{7,6},{8,9},{9,8},{10,11... | collective-permute-start | bytes 6291464 | tf_op jit(solution)/shard_map/ppermute | solution.py:338
  0.5 3.9 %deposit.1 = (f32[4,16,128]{2,1,0:T(8,128)S(1)}, bf16[32,8,2048]{2,1,0:T(8,128)(2,1)S(1)}) custom-call(s32[1,256,256]{2,1,0:T(8,128)} %cyc_at.1, s32[1,256,256]{2,1,0:T(8,128)} %pix_at.1, f32[1,256,256]{2,1,0:T(8,128)} %mass_at.1, s32[1,256]{1,0:T(1,128)} %place_at.1, s32[1,256]{1,0:T(1,128)} %shell_at.1, s32[1,256]{1,0:T(1,128)} %bitcast.24, ...), custom_call_target="tpu_custom_call" | custom-call | tf_op jit(solution)/shard_map/deposit/pallas_call | solution.py:273
  4.4 0.1 collective-permute-start.1
  4.4 1.2 %collective-permute-done.1 = f32[4,16,128]{2,1,0:T(8,128)S(1)} collective-permute-done((f32[4,16,128]{2,1,0:T(8,128)S(1)}, f32[4,16,128]{2,1,0:T(8,128)S(1)}, u32[]{:S(2)}, u32[]{:S(2)}) %collective-permute-start.1) | collective-permute-done | bytes 32800 | tf_op jit(solution)/shard_map/ppermute | solution.py:174
  5.6 2.8 %collective-permute-start.2 = (f32[2,16,128]{2,1,0:T(8,128)S(1)}, f32[2,16,128]{2,1,0:T(8,128)S(1)}, u32[]{:S(2)}, u32[]{:S(2)}) collective-permute-start(f32[2,16,128]{2,1,0:T(8,128)S(1)} %slice_bitcast_fusion), channel_id=1, source_target_pairs={{0,4},{1,5},{2,6},{3,7},{4,0},{5,1},{6,2},{7,3},{8,12},{9,13},{10,... | collective-permute-start | bytes 49160 | tf_op jit(solution)/shard_map/ppermute | solution.py:174
  8.4 1.7 %collective-permute-done.2 = f32[2,16,128]{2,1,0:T(8,128)S(1)} collective-permute-done((f32[2,16,128]{2,1,0:T(8,128)S(1)}, f32[2,16,128]{2,1,0:T(8,128)S(1)}, u32[]{:S(2)}, u32[]{:S(2)}) %collective-permute-start.2) | collective-permute-done | bytes 16416 | tf_op jit(solution)/shard_map/ppermute | solution.py:174
  10.2 3.0 %collective-permute-start.3 = (f32[1,16,128]{2,1,0:T(8,128)S(1)}, f32[1,16,128]{2,1,0:T(8,128)S(1)}, u32[]{:S(2)}, u32[]{:S(2)}) collective-permute-start(f32[1,16,128]{2,1,0:T(8,128)S(1)} %slice_bitcast_fusion.2), channel_id=1, source_target_pairs={{0,8},{1,9},{2,10},{3,11},{4,12},{5,13},{6,14},{7,15},{8,0},{9,1},... | collective-permute-start | bytes 24584 | tf_op jit(solution)/shard_map/ppermute | solution.py:174
  13.2 1.6 %collective-permute-done.3 = f32[1,16,128]{2,1,0:T(8,128)S(1)} collective-permute-done((f32[1,16,128]{2,1,0:T(8,128)S(1)}, f32[1,16,128]{2,1,0:T(8,128)S(1)}, u32[]{:S(2)}, u32[]{:S(2)}) %collective-permute-start.3) | collective-permute-done | bytes 8224 | tf_op jit(solution)/shard_map/ppermute | solution.py:174
  14.8 1.8 %collective-permute-start.4 = (f32[1,16,128]{2,1,0:T(8,128)S(1)}, f32[1,16,128]{2,1,0:T(8,128)S(1)}, u32[]{:S(2)}, u32[]{:S(2)}) collective-permute-start(f32[1,16,128]{2,1,0:T(8,128)S(1)} %fusion.2.refs_0_), channel_id=1, source_target_pairs={{0,2},{1,3},{2,0},{3,1},{4,6},{5,7},{6,4},{7,5},{8,10},{9,11},{10,... | collective-permute-start | bytes 24584 | tf_op jit(solution)/shard_map/ppermute | solution.py:174
  16.6 1.8 %collective-permute-done.4.refs_1_ = f32[1,16,128]{2,1,0:T(8,128)S(1)} collective-permute-done((f32[1,16,128]{2,1,0:T(8,128)S(1)}, f32[1,16,128]{2,1,0:T(8,128)S(1)}, u32[]{:S(2)}, u32[]{:S(2)}) %collective-permute-start.4) | collective-permute-done | bytes 8224 | tf_op jit(solution)/shard_map/ppermute | solution.py:174
  18.5 0.0 collective-permute-done.other
  18.5 0.0 copy-done
  18.5 2.3 %legendre.1 = f32[2,32,2,2048]{3,2,1,0:T(2,128)} custom-call(f32[4,4]{1,0:T(4,128)S(1)} %copy-done, bf16[32,8,2048]{2,1,0:T(8,128)(2,1)S(1)} %get-tuple-element.7.own, bf16[32,8,4096]{2,1,0:T(8,128)(2,1)S(1)} %collective-permute-done.other, f32[1,16,128]{2,1,0:T(8,128)S(1)} %fusion.2.refs_0_, f32[1,16,128]{2,1,0:T(8,128)S(1)} %collective-permute-done.4.refs_1_), custom_call_target="tpu_custom_call" | custom-call | tf_op jit(solution)/shard_map/legendre/pallas_call | solution.py:318
  (5 shorter events, 0.0 us)
Async XLA Ops:
  0.0 18.5 %copy-start = (f32[4,4]{1,0:T(4,128)S(1)}, f32[4,4]{1,0:T(4,128)}, u32[]{:S(2)}) copy-start(f32[4,4]{1,0:T(4,128)} %weight.1) | copy-start | bytes 196
  0.0 18.5 %collective-permute-start = (bf16[32,8,4096]{2,1,0:T(8,128)(2,1)}, bf16[32,8,4096]{2,1,0:T(8,128)(2,1)S(1)}, u32[]{:S(2)}, u32[]{:S(2)}) collective-permute-start(bf16[32,8,4096]{2,1,0:T(8,128)(2,1)} %basis.1), channel_id=1, source_target_pairs={{0,1},{1,0},{2,3},{3,2},{4,5},{5,4},{6,7},{7,6},{8,9},{9,8},{10,11... | collective-permute-start | bytes 6291464 | tf_op jit(solution)/shard_map/ppermute | solution.py:338
  4.4 1.3 %collective-permute-start.1 = (f32[4,16,128]{2,1,0:T(8,128)S(1)}, f32[4,16,128]{2,1,0:T(8,128)S(1)}, u32[]{:S(2)}, u32[]{:S(2)}) collective-permute-start(f32[4,16,128]{2,1,0:T(8,128)S(1)} %get-tuple-element.8), channel_id=1, source_target_pairs={{0,1},{1,0},{2,3},{3,2},{4,5},{5,4},{6,7},{7,6},{8,9},{9,8},{10,11... | collective-permute-start | bytes 98312 | tf_op jit(solution)/shard_map/ppermute | solution.py:174
  5.6 4.5 %collective-permute-start.2 = (f32[2,16,128]{2,1,0:T(8,128)S(1)}, f32[2,16,128]{2,1,0:T(8,128)S(1)}, u32[]{:S(2)}, u32[]{:S(2)}) collective-permute-start(f32[2,16,128]{2,1,0:T(8,128)S(1)} %slice_bitcast_fusion), channel_id=1, source_target_pairs={{0,4},{1,5},{2,6},{3,7},{4,0},{5,1},{6,2},{7,3},{8,12},{9,13},{10,... | collective-permute-start | bytes 49160 | tf_op jit(solution)/shard_map/ppermute | solution.py:174
  10.2 4.7 %collective-permute-start.3 = (f32[1,16,128]{2,1,0:T(8,128)S(1)}, f32[1,16,128]{2,1,0:T(8,128)S(1)}, u32[]{:S(2)}, u32[]{:S(2)}) collective-permute-start(f32[1,16,128]{2,1,0:T(8,128)S(1)} %slice_bitcast_fusion.2), channel_id=1, source_target_pairs={{0,8},{1,9},{2,10},{3,11},{4,12},{5,13},{6,14},{7,15},{8,0},{9,1},... | collective-permute-start | bytes 24584 | tf_op jit(solution)/shard_map/ppermute | solution.py:174
  14.8 3.7 %collective-permute-start.4 = (f32[1,16,128]{2,1,0:T(8,128)S(1)}, f32[1,16,128]{2,1,0:T(8,128)S(1)}, u32[]{:S(2)}, u32[]{:S(2)}) collective-permute-start(f32[1,16,128]{2,1,0:T(8,128)S(1)} %fusion.2.refs_0_), channel_id=1, source_target_pairs={{0,2},{1,3},{2,0},{3,1},{4,6},{5,7},{6,4},{7,5},{8,10},{9,11},{10,... | collective-permute-start | bytes 24584 | tf_op jit(solution)/shard_map/ppermute | solution.py:174

commit v4 on v3

--- a/solution.py
+++ b/solution.py
@@ -8,6 +8,7 @@
 from jax.experimental import pallas as pl
 from jax.experimental.pallas import tpu as pltpu
 from jax.sharding import PartitionSpec as P
+
 
 NP = 8192
 M = 128
@@ -155,13 +156,6 @@
 SPAN = 512
 
 
-def stages_of(sky, shells):
-    bits = [("sub", 1)]
-    bits += [("sky", 1 << i) for i in range(sky.bit_length() - 1)]
-    bits += [("shell", 1 << i) for i in range(shells.bit_length() - 1)]
-    return [[bit] for bit in bits]
-
-
 AXES = ("sky", "shell", "sub")
 
 
@@ -170,92 +164,76 @@
     pairs = []
     for here in np.ndindex(*sizes):
         there = [i ^ change.get(a, 0) for a, i in zip(AXES, here)]
+        there[2] = sizes[2] - 1 - here[2]
         pairs.append((int(np.ravel_multi_index(here, sizes)), int(np.ravel_multi_index(there, sizes))))
     return lax.ppermute(x, AXES, pairs)
 
 
-def exchange(y, stages):
-    groups = {0: y}
-    for number, steps in enumerate(stages):
-        last = number == len(stages) - 1
-        skies = [bit for axis, bit in steps if axis == "sky"]
-        width = len(skies)
-        fresh = {}
-        for g, value in groups.items():
-            rest = value.shape[1:]
-            value = value.reshape((-1,) + (2,) * width + rest)
-            for chosen in range(1 << len(steps)):
-                change, index, target = {}, [slice(None)] + [0] * width, g
-                for i, (axis, bit) in enumerate(steps):
-                    if chosen >> i & 1:
-                        change[axis] = change.get(axis, 0) ^ bit
-                        if axis == "sky":
-                            index[width - skies.index(bit)] = 1
-                        if axis == "shell":
-                            target ^= bit
-                piece = value[tuple(index)]
-                fresh.setdefault(target, []).append(swap(piece, change) if change else piece)
-        if last:
-            return [fresh[g] for g in sorted(fresh)]
-        groups = {g: sum(pieces[1:], pieces[0]) for g, pieces in fresh.items()}
-
-
-def legendre_kernel(weight, own, other, *refs, counts, blocks):
+def exchange(y):
+    y = y + swap(y, {})
+    bit = 1
+    while y.shape[0] > 1:
+        y = y.reshape(-1, 2, *y.shape[1:])
+        given = swap(y[:, 1], {"sky": bit})
+        y = y[:, 0] + given
+        bit *= 2
+    parts, bit = [y], 1
+    while bit < lax.axis_size("shell"):
+        parts = parts + [swap(p, {"shell": bit}) for p in parts]
+        bit *= 2
+    return parts
+
+
+def legendre_kernel(weight, own, other, *refs, blocks):
     refs, (out, left, result, sems) = refs[:-4], refs[-4:]
+    orders, cycles, degrees = own.shape
     lanes = refs[0].shape[-1]
-    orders = own.shape[0]
-    cycles = own.shape[1]
-    width = orders * cycles
-    half = lanes // CYCLE_DEV
-    planes = result.shape[0]
+    planes = out.shape[0]
+    some = orders // 2
+    width = 2 * some * cycles
     sub, place = lax.axis_index("sub"), lax.axis_index("shell")
 
     first = place * planes
     maps = []
-    for x, count in enumerate(counts):
-        at = sum(counts[:x])
-        total = refs[at][0]
-        for i in range(1, count):
-            total = total + refs[at + i][0]
-        total = (total * (2.0 * math.pi / NP)).astype(bf16).astype(f32)
+    for x, ref in enumerate(refs):
+        total = (ref[0] * (2.0 * math.pi / NP)).astype(bf16).astype(f32)
         maps += [
-            ((place ^ x) * SHELL_DEV + s, total[s * blocks : (s + 1) * blocks])
-            for s in range(SHELL_DEV)
+            ((place ^ x) * SHELL_DEV + s, total[s * blocks : (s + 1) * blocks]) for s in range(SHELL_DEV)
         ]
     column = lax.broadcasted_iota(jnp.int32, (blocks, width), 1)
     row = lax.broadcasted_iota(jnp.int32, (blocks, width), 0)
+    mine = jnp.where(column < width // 2, sub, 1 - sub)
+    spread = jnp.where(row == (mine * cycles + column % cycles) // CYCLE_DEV, 1.0, 0.0).astype(bf16)
+    half = 2 * some
     wide = lax.broadcasted_iota(jnp.int32, (half, width), 1)
-    keep = lax.broadcasted_iota(jnp.int32, (half, width), 0) // 2 == wide // cycles
+    keep = lax.broadcasted_iota(jnp.int32, (half, width), 0) // 2 == wide % (width // 2) // cycles
     even = wide % CYCLE_DEV == 0
-    for side in range(2):
-        mine = sub if side == 0 else 1 - sub
-        cycle = mine * cycles + column % cycles
-        spread = jnp.where(row == cycle // CYCLE_DEV, 1.0, 0.0).astype(bf16)
-        for i in range(planes):
-            total = jnp.zeros((blocks, lanes), f32)
-            for s, value in maps:
-                factor = jnp.where(s <= first + i, weight[first + i, s], 0.0)
-                total = total + factor * value
-            high, low = split(total)
-            for j, piece in enumerate((high, low)):
-                grown = dot(piece, spread, ((0,), (0,)))
-                grown = jnp.where(even, grown[:half], grown[half:])
-                grown = jnp.where(keep, grown, 0.0).astype(bf16)
+    for i in range(planes):
+        total = jnp.zeros((blocks, lanes), f32)
+        for s, value in maps:
+            factor = jnp.where(s <= first + i, weight[first + i, s], 0.0)
+            total = total + factor * value
+        for j, piece in enumerate(split(total)):
+            grown = dot(piece, spread, ((0,), (0,)))
+            for h in range(2):
+                value = jnp.where(even, grown[h * half : (h + 1) * half], grown[(2 + h) * half : (3 + h) * half])
                 start = (j * planes + i) * half
-                left[side, start : start + half, :] = grown
+                left[h, start : start + half, :] = jnp.where(keep, value, 0.0).astype(bf16)
 
     copies = []
-    for step in range(own.shape[2] // SPAN):
+    for step in range(degrees // SPAN):
         at = pl.ds(step * SPAN, SPAN)
-        far = pl.ds(pl.multiple_of(sub * own.shape[2] + step * SPAN, 128), SPAN)
-        a = own[:, :, at].reshape(width, SPAN)
-        b = other[:, :, far].reshape(width, SPAN)
-        value = dot(left[0], a) + dot(left[1], b)
-        value = value[: planes * half] + value[planes * half :]
-        for i in range(planes):
-            for m in range(orders):
-                start = i * half + m * 2
-                result[i, m, :, at] = value[start : start + 2, :]
+        far = pl.ds(pl.multiple_of(sub * degrees + step * SPAN, 128), SPAN)
+        for h in range(2):
+            here = slice(h * some, (h + 1) * some)
+            a = own[here, :, at].reshape(width // 2, SPAN)
+            b = other[here, :, far].reshape(width // 2, SPAN)
+            value = dot(left[h], jnp.concatenate([a, b], 0))
+            value = value[: planes * half] + value[planes * half :]
+            for i in range(planes):
+                for m in range(some):
+                    start = i * half + m * 2
+                    result[i, h * some + m, :, at] = value[start : start + 2, :]
         copies.append(pltpu.make_async_copy(result.at[:, :, :, at], out.at[:, :, :, at], sems.at[step]))
         copies[-1].start()
     for copy in copies:
@@ -313,21 +291,20 @@
 
 def legendre_call(lens_weight, own, other, parts, planes, blocks):
     orders, cycles, degrees = own.shape
-    flat = [piece for group in parts for piece in group]
     vmem = pl.BlockSpec(memory_space=pltpu.VMEM)
     return pl.pallas_call(
-        functools.partial(legendre_kernel, counts=[len(group) for group in parts], blocks=blocks),
+        functools.partial(legendre_kernel, blocks=blocks),
         out_shape=jax.ShapeDtypeStruct((planes, orders, 2, degrees), f32),
-        in_specs=[pl.BlockSpec(memory_space=pltpu.SMEM), vmem, vmem] + [vmem] * len(flat),
+        in_specs=[pl.BlockSpec(memory_space=pltpu.SMEM), vmem, vmem] + [vmem] * len(parts),
         out_specs=pl.BlockSpec(memory_space=pltpu.HBM),
         scratch_shapes=[
-            pltpu.VMEM((2, 4 * planes * orders, orders * cycles), bf16),
+            pltpu.VMEM((2, 2 * planes * orders, orders * cycles), bf16),
             pltpu.VMEM((planes, orders, 2, degrees), f32),
             pltpu.SemaphoreType.DMA((degrees // SPAN,)),
         ],
         compiler_params=pltpu.CompilerParams(vmem_limit_bytes=LIMIT),
         name="legendre",
-    )(lens_weight, own, other, *flat)
+    )(lens_weight, own, other, *parts)
 
 
 def body(part_cycle, part_pixel, part_mass, tile_block, tile_shell, tile_pixel, basis, lens_weight):
@@ -335,7 +312,7 @@
     tiles = part_cycle.shape[1]
     _, cycles, degrees = basis.shape
     blocks = cycles * sub // CYCLE_DEV
-    other = lax.ppermute(basis, "sub", [(i, (i + 1) % sub) for i in range(sub)])
+    other = swap(basis, {})
     send, own = deposit_call(
         part_cycle,
         part_pixel,
@@ -348,7 +325,7 @@
         blocks,
         degrees // sub,
     )
-    parts = exchange(send, stages_of(sky, shells))
+    parts = exchange(send)
     return legendre_call(lens_weight, own, other, parts, lens_weight.shape[0] // shells, blocks)
 
 

time: 21 us -> 19.2 us (0.914)
  waiting for transfers between devices: 6.37 us -> 5.57 us
  starting transfers between devices: 8.21 us -> 7.56 us
  Pallas kernels: 6.18 us -> 5.9 us
    ppermute x4 -> x5, waiting for transfers between devices: 6.36 us -> 5.57 us  [swap(): return lax.ppermute(x, AXES, pairs)]
    ppermute x1 -> x0, starting transfers between devices: 0.49 us -> none  [body(): other = lax.ppermute(basis, 'sub', [(i, (i + 1) % sub) for i in range(sub)])]
    pallas_call x1, Pallas kernels: 2.33 us -> 2.05 us  [legendre_call(): pl.pallas_call(functools.partial(legendre_kernel, blocks=blocks), out_sha...]
    ppermute x4 -> x5, starting transfers between devices: 7.72 us -> 7.56 us  [swap(): return lax.ppermute(x, AXES, pairs)]
  transfers between devices with their start and end apart: 5 -> 5, of which waited for: 4 -> 4; matrix products, arithmetic and copies ran while one was open for 0% -> 0% of each run, Pallas kernels for 19% -> 20%
where the time goes in v4:
time: 19.2 us; the launch traced here: 19.1 us
  starting transfers between devices  7.56 us (39%)
  Pallas kernels  5.9 us (31%)
  waiting for transfers between devices  5.57 us (29%)
    ppermute x5, starting transfers between devices, swap(): return lax.ppermute(x, AXES, pairs)  7.56 us
    ppermute x5, waiting for transfers between devices, swap(): return lax.ppermute(x, AXES, pairs)  5.57 us
    pallas_call x1, Pallas kernels, deposit_call(): pl.pallas_call(functools.partial(deposit_kernel, blocks=blocks), out_shap...  3.86 us
    pallas_call x1, Pallas kernels, legendre_call(): pl.pallas_call(functools.partial(legendre_kernel, blocks=blocks), out_sha...  2.05 us
  transfers between devices with their start and end apart: 5, of which 4 were waited for; matrix products, arithmetic and copies ran while one was open for 0% of the time, Pallas kernels for 20%

profile of v4, /device:TPU:0, one launch (start us, length us, event | category | flops | bytes accessed | tf_op | source)
XLA Modules:
  0.0 19.1 jit_solution(17003583485747286814)
XLA Ops:
  0.0 0.0 copy-start
  0.0 0.5 %collective-permute-start = (bf16[32,8,4096]{2,1,0:T(8,128)(2,1)}, bf16[32,8,4096]{2,1,0:T(8,128)(2,1)S(1)}, u32[]{:S(2)}, u32[]{:S(2)}) collective-permute-start(bf16[32,8,4096]{2,1,0:T(8,128)(2,1)} %basis.1), channel_id=1, source_target_pairs={{0,1},{1,0},{2,3},{3,2},{4,5},{5,4},{6,7},{7,6},{8,9},{9,8},{10,11... | collective-permute-start | bytes 6291464 | tf_op jit(solution)/shard_map/ppermute | solution.py:169
  0.5 3.9 %deposit.1 = (f32[4,16,128]{2,1,0:T(8,128)S(1)}, bf16[32,8,2048]{2,1,0:T(8,128)(2,1)S(1)}) custom-call(s32[1,256,256]{2,1,0:T(8,128)} %cyc_at.1, s32[1,256,256]{2,1,0:T(8,128)} %pix_at.1, f32[1,256,256]{2,1,0:T(8,128)} %mass_at.1, s32[1,256]{1,0:T(1,128)} %place_at.1, s32[1,256]{1,0:T(1,128)} %shell_at.1, s32[1,256]{1,0:T(1,128)} %bitcast.24, ...), custom_call_target="tpu_custom_call" | custom-call | tf_op jit(solution)/shard_map/deposit/pallas_call | solution.py:251
  4.4 0.1 collective-permute-start.1
  4.4 1.2 %collective-permute-done.1 = f32[4,16,128]{2,1,0:T(8,128)S(1)} collective-permute-done((f32[4,16,128]{2,1,0:T(8,128)S(1)}, f32[4,16,128]{2,1,0:T(8,128)S(1)}, u32[]{:S(2)}, u32[]{:S(2)}) %collective-permute-start.1) | collective-permute-done | bytes 32800 | tf_op jit(solution)/shard_map/ppermute | solution.py:169
  5.6 2.7 %collective-permute-start.2 = (f32[2,16,128]{2,1,0:T(8,128)S(1)}, f32[2,16,128]{2,1,0:T(8,128)S(1)}, u32[]{:S(2)}, u32[]{:S(2)}) collective-permute-start(f32[2,16,128]{2,1,0:T(8,128)S(1)} %slice_bitcast_fusion), channel_id=1, source_target_pairs={{0,5},{1,4},{2,7},{3,6},{4,1},{5,0},{6,3},{7,2},{8,13},{9,12},{10,... | collective-permute-start | bytes 49160 | tf_op jit(solution)/shard_map/ppermute | solution.py:169
  8.4 1.4 %collective-permute-done.2 = f32[2,16,128]{2,1,0:T(8,128)S(1)} collective-permute-done((f32[2,16,128]{2,1,0:T(8,128)S(1)}, f32[2,16,128]{2,1,0:T(8,128)S(1)}, u32[]{:S(2)}, u32[]{:S(2)}) %collective-permute-start.2) | collective-permute-done | bytes 16416 | tf_op jit(solution)/shard_map/ppermute | solution.py:169
  9.8 2.7 %collective-permute-start.3 = (f32[1,16,128]{2,1,0:T(8,128)S(1)}, f32[1,16,128]{2,1,0:T(8,128)S(1)}, u32[]{:S(2)}, u32[]{:S(2)}) collective-permute-start(f32[1,16,128]{2,1,0:T(8,128)S(1)} %slice_bitcast_fusion.2), channel_id=1, source_target_pairs={{0,9},{1,8},{2,11},{3,10},{4,13},{5,12},{6,15},{7,14},{8,1},{9,0},... | collective-permute-start | bytes 24584 | tf_op jit(solution)/shard_map/ppermute | solution.py:169
  12.6 1.4 %collective-permute-done.3 = f32[1,16,128]{2,1,0:T(8,128)S(1)} collective-permute-done((f32[1,16,128]{2,1,0:T(8,128)S(1)}, f32[1,16,128]{2,1,0:T(8,128)S(1)}, u32[]{:S(2)}, u32[]{:S(2)}) %collective-permute-start.3) | collective-permute-done | bytes 8224 | tf_op jit(solution)/shard_map/ppermute | solution.py:169
  13.9 1.5 %collective-permute-start.4 = (f32[1,16,128]{2,1,0:T(8,128)S(1)}, f32[1,16,128]{2,1,0:T(8,128)S(1)}, u32[]{:S(2)}, u32[]{:S(2)}) collective-permute-start(f32[1,16,128]{2,1,0:T(8,128)S(1)} %fusion.2.refs_0_), channel_id=1, source_target_pairs={{0,3},{1,2},{2,1},{3,0},{4,7},{5,6},{6,5},{7,4},{8,11},{9,10},{10,... | collective-permute-start | bytes 24584 | tf_op jit(solution)/shard_map/ppermute | solution.py:169
  15.5 1.6 %collective-permute-done.4.refs_1_ = f32[1,16,128]{2,1,0:T(8,128)S(1)} collective-permute-done((f32[1,16,128]{2,1,0:T(8,128)S(1)}, f32[1,16,128]{2,1,0:T(8,128)S(1)}, u32[]{:S(2)}, u32[]{:S(2)}) %collective-permute-start.4) | collective-permute-done | bytes 8224 | tf_op jit(solution)/shard_map/ppermute | solution.py:169
  17.0 0.0 collective-permute-done.other
  17.0 0.0 copy-done
  17.0 2.0 %legendre.1 = f32[2,32,2,2048]{3,2,1,0:T(2,128)} custom-call(f32[4,4]{1,0:T(4,128)S(1)} %copy-done, bf16[32,8,2048]{2,1,0:T(8,128)(2,1)S(1)} %get-tuple-element.7.own, bf16[32,8,4096]{2,1,0:T(8,128)(2,1)S(1)} %collective-permute-done.other, f32[1,16,128]{2,1,0:T(8,128)S(1)} %fusion.2.refs_0_, f32[1,16,128]{2,1,0:T(8,128)S(1)} %collective-permute-done.4.refs_1_), custom_call_target="tpu_custom_call" | custom-call | tf_op jit(solution)/shard_map/legendre/pallas_call | solution.py:295
  (5 shorter events, 0.0 us)
Async XLA Ops:
  0.0 17.0 %copy-start = (f32[4,4]{1,0:T(4,128)S(1)}, f32[4,4]{1,0:T(4,128)}, u32[]{:S(2)}) copy-start(f32[4,4]{1,0:T(4,128)} %weight.1) | copy-start | bytes 196
  0.0 17.0 %collective-permute-start = (bf16[32,8,4096]{2,1,0:T(8,128)(2,1)}, bf16[32,8,4096]{2,1,0:T(8,128)(2,1)S(1)}, u32[]{:S(2)}, u32[]{:S(2)}) collective-permute-start(bf16[32,8,4096]{2,1,0:T(8,128)(2,1)} %basis.1), channel_id=1, source_target_pairs={{0,1},{1,0},{2,3},{3,2},{4,5},{5,4},{6,7},{7,6},{8,9},{9,8},{10,11... | collective-permute-start | bytes 6291464 | tf_op jit(solution)/shard_map/ppermute | solution.py:169
  4.4 1.3 %collective-permute-start.1 = (f32[4,16,128]{2,1,0:T(8,128)S(1)}, f32[4,16,128]{2,1,0:T(8,128)S(1)}, u32[]{:S(2)}, u32[]{:S(2)}) collective-permute-start(f32[4,16,128]{2,1,0:T(8,128)S(1)} %get-tuple-element.8), channel_id=1, source_target_pairs={{0,1},{1,0},{2,3},{3,2},{4,5},{5,4},{6,7},{7,6},{8,9},{9,8},{10,11... | collective-permute-start | bytes 98312 | tf_op jit(solution)/shard_map/ppermute | solution.py:169
  5.6 4.2 %collective-permute-start.2 = (f32[2,16,128]{2,1,0:T(8,128)S(1)}, f32[2,16,128]{2,1,0:T(8,128)S(1)}, u32[]{:S(2)}, u32[]{:S(2)}) collective-permute-start(f32[2,16,128]{2,1,0:T(8,128)S(1)} %slice_bitcast_fusion), channel_id=1, source_target_pairs={{0,5},{1,4},{2,7},{3,6},{4,1},{5,0},{6,3},{7,2},{8,13},{9,12},{10,... | collective-permute-start | bytes 49160 | tf_op jit(solution)/shard_map/ppermute | solution.py:169
  9.8 4.1 %collective-permute-start.3 = (f32[1,16,128]{2,1,0:T(8,128)S(1)}, f32[1,16,128]{2,1,0:T(8,128)S(1)}, u32[]{:S(2)}, u32[]{:S(2)}) collective-permute-start(f32[1,16,128]{2,1,0:T(8,128)S(1)} %slice_bitcast_fusion.2), channel_id=1, source_target_pairs={{0,9},{1,8},{2,11},{3,10},{4,13},{5,12},{6,15},{7,14},{8,1},{9,0},... | collective-permute-start | bytes 24584 | tf_op jit(solution)/shard_map/ppermute | solution.py:169
  13.9 3.1 %collective-permute-start.4 = (f32[1,16,128]{2,1,0:T(8,128)S(1)}, f32[1,16,128]{2,1,0:T(8,128)S(1)}, u32[]{:S(2)}, u32[]{:S(2)}) collective-permute-start(f32[1,16,128]{2,1,0:T(8,128)S(1)} %fusion.2.refs_0_), channel_id=1, source_target_pairs={{0,3},{1,2},{2,1},{3,0},{4,7},{5,6},{6,5},{7,4},{8,11},{9,10},{10,... | collective-permute-start | bytes 24584 | tf_op jit(solution)/shard_map/ppermute | solution.py:169
